TPU v7x, 256 devices: a whole 4x4x8 slice. The times are simulated.
256 devices in a mesh: tile: 4 (over z_lo, core), freq: 64 (over y, z_hi, x).
Axes of the slice: x: 4, y: 4, z: 8 (z_hi: 4, z_lo: 2; z = z_hi * 2 + z_lo), core: 2. Of those that a mesh axis runs over, the one named last changes fastest.
Arguments:
- sky: bfloat16 [4, 512, 2, 4096], P('tile', 'freq'), may hold values from -6 to 6
- kernel: bfloat16 [4, 64, 2, 4096, 128], P('tile', 'freq'), may hold values from -0.0625 to 0.0625
- data: bfloat16 [64, 2, 128, 512], P('freq'), may hold values from -6 to 6
- block_tiles: int32 [64, 4], P('freq'), may hold values 0 or 1
- length_bin: int32 [64, 128], P('freq'), may hold values from 0 to 31
- wedge_keep: int32 [32, 512], replicated, may hold values 0 or 1
Outputs:
- gradient: float32 [4, 512, 2, 4096], P('tile', 'freq')
All inputs are finite; a program needn't handle non-finite values. No bound on the sum of `block_tiles` on one device may be relied on, other than what follows from the above.
Results may differ from a plain program's by a relative error of at most 0.0027.
Values may be sent and summed in bfloat16 or wider, within the bound.
A program may use at most 128 MiB of HBM per device.

v0:
```python
import math

import jax
import jax.numpy as jnp
from jax import lax
from jax.sharding import Mesh
from jax.sharding import PartitionSpec as P

FREQ = ("freq_0", "freq_1", "freq_2")


def sent_to_all(shard, axis):
    copies = jnp.broadcast_to(shard, (lax.axis_size(axis), *shard.shape))
    return lax.all_to_all(copies, axis, split_axis=0, concat_axis=0, tiled=True)


def of_everyone(shard, axis):
    return sent_to_all(shard, axis).sum(axis=0)


def own_block(tiles, axes, sequence):
    dims = [lax.axis_size(a) for a in axes]
    tiles = tiles.reshape(*dims, *tiles.shape[1:])
    tiles = tiles.transpose(*sequence, *range(len(axes), tiles.ndim))
    tiles = tiles.reshape(-1, *tiles.shape[len(axes) :])
    for k in sequence:
        tiles = lax.psum_scatter(tiles, axes[k], scatter_dimension=0, tiled=True)
    return tiles[0]


def in_blocks(shard, dim, count):
    before, after = (shard.shape[:dim], shard.shape[dim + 1 :])
    return jnp.moveaxis(shard.reshape(*before, count, -1, *after), dim, 0)


def scatter_axes(shard, axes, sequence, dim):
    count = lax.axis_size(axes)
    return own_block(in_blocks(shard, dim, count), axes, sequence)


def delay_tables(length):
    indices = jnp.arange(length, dtype=jnp.int32)
    product = indices[:, None] * indices[None, :] % length
    angle = product.astype(jnp.float32) * (2.0 * math.pi / length)
    return (jnp.cos(angle), jnp.sin(angle))


def real_form(kernel_pair):
    upper_half = jnp.concatenate([kernel_pair[0], kernel_pair[1]], axis=1)
    lower_half = jnp.concatenate([-kernel_pair[1], kernel_pair[0]], axis=1)
    return jnp.concatenate([upper_half, lower_half], axis=0)


def transform(values, table):
    return jnp.einsum("...c,ck->...k", values, table, precision=lax.Precision.HIGHEST)


def keep_table(own_bins, wedge_keep):
    levels = jnp.arange(wedge_keep.shape[0], dtype=jnp.int32)
    one_hot = (own_bins[:, :, None] == levels[None, None, :]).astype(jnp.float32)
    return jnp.einsum(
        "jbl,lk->jbk", one_hot, wedge_keep.astype(jnp.float32), precision=lax.Precision.HIGHEST
    )


def back_project(visibility, data, keep_mask, cosine, sine_table):
    norm_factor = 1.0 / math.sqrt(cosine.shape[0])
    real_vis = visibility[:, 0]
    imag_vis = visibility[:, 1]
    spec_real = (transform(real_vis, cosine) + transform(imag_vis, sine_table)) * norm_factor
    spec_imag = (transform(imag_vis, cosine) - transform(real_vis, sine_table)) * norm_factor
    miss_real = keep_mask * (spec_real - data[:, 0].astype(jnp.float32))
    miss_imag = keep_mask * (spec_imag - data[:, 1].astype(jnp.float32))
    back_real = (transform(miss_real, cosine) - transform(miss_imag, sine_table)) * norm_factor
    back_imag = (transform(miss_imag, cosine) + transform(miss_real, sine_table)) * norm_factor
    return jnp.stack([back_real, back_imag], axis=1).astype(jnp.bfloat16)


def body(sky, kernel, data, block_tiles, length_bin, wedge_keep):
    channels = data.shape[3]
    blocks = kernel.shape[1]
    cell_count = kernel.shape[3]
    base_count = kernel.shape[4]
    local_channels = sky.shape[1]
    tile_pos = lax.axis_index("tile")
    column = jnp.arange(block_tiles.shape[1], dtype=jnp.int32) == tile_pos
    weights = jnp.sum(jnp.where(column[None, :], block_tiles, 0), axis=1).astype(jnp.float32)
    real_forms = jax.vmap(real_form)(kernel[0])
    sky_piece = lax.all_gather(sky, FREQ, axis=1, tiled=True)
    flat_rows = sky_piece[0].reshape(sky_piece.shape[1], 2 * cell_count)
    visibility = jnp.einsum(
        "nc,jcb->jbn", flat_rows, real_forms, preferred_element_type=jnp.float32
    )
    partial_vis = visibility * weights[:, None, None]
    cosine, sine_table = delay_tables(channels)
    visibility = of_everyone(partial_vis, "tile").reshape(blocks, 2, base_count, channels)
    back_field = back_project(
        visibility, data, keep_table(length_bin, wedge_keep), cosine, sine_table
    )
    scaled = (back_field * weights[:, None, None, None].astype(jnp.bfloat16)).reshape(
        blocks, 2 * base_count, channels
    )
    partial_value = jnp.einsum(
        "jpn,jcp->nc", scaled, real_forms, preferred_element_type=jnp.float32
    )
    gradient = scatter_axes(
        partial_value.reshape(local_channels * lax.axis_size(FREQ), 2, cell_count),
        FREQ,
        (0, 2, 1),
        0,
    )
    return gradient[None]


def solution(mesh):
    finer = Mesh(
        mesh.devices.reshape(mesh.shape["tile"], 4, 4, 4), ("tile", "freq_0", "freq_1", "freq_2")
    )
    return jax.shard_map(
        body,
        mesh=finer,
        in_specs=(
            P("tile", FREQ, None, None),
            P("tile", FREQ, None, None, None),
            P(FREQ, None, None, None),
            P(FREQ, None),
            P(FREQ, None),
            P(),
        ),
        out_specs=P("tile", FREQ, None, None),
        check_vma=False,
    )
```

profile of v0, /device:TPU:8, one launch (start us, length us, event | category | flops | bytes accessed | tf_op | source)
XLA Modules:
  0.0 477.6 jit_solution(9158189896188263960)
XLA Ops:
  6.5 0.0 all-gather.2.cloned.1.call-start
  6.5 0.7 all-gather.2.cloned.1.call-update
  7.3 1.3 fusion.40
  9.2 1.4 fusion.73
  10.6 1.7 slice_bitcast_fusion
  12.3 0.0 copy-start
  12.3 0.0 copy-start.1
  12.3 108.5 %all-gather.2.cloned.1.call-done = bf16[1,512,2,4096]{3,2,0,1:T(2,128)(2,1)} async-done(((bf16[1,8,2,4096]{3,2,0,1:T(2,128)(2,1)}), bf16[1,512,2,4096]{3,2,0,1:T(2,128)(2,1)}) %all-gather.2.cloned.1.call-update) | async-done | bytes 8388624 | tf_op jit(solution)/shard_map/all_gather | solution.py:89
  120.7 16.2 %copy.21 = bf16[64,8,2,4096]{3,1,2,0:T(8,128)(2,1)} copy(bf16[64,8,2,4096]{3,2,1,0:T(2,128)(2,1)} %bitcast.61) | data formatting | bytes 16777216
  136.9 0.0 copy-done
  136.9 0.0 copy-done.1
  137.0 0.0 copy-start.2
  137.0 0.0 copy-start.3
  137.0 6.3 %fusion.2 = f32[256,512]{1,0:T(8,128)S(1)} fusion(bf16[512,8192]{1,0:T(8,128)(2,1)} %bitcast.62, f32[]{:T(128)S(6)} %convert_element_type.51, bf16[1,4096,128]{2,1,0:T(8,128)(2,1)S(1)} %get-tuple-element.6, bf16[1,4096,128]{2,1,0:T(8,128)(2,1)S(1)} %fusion.73, bf16[1,4096,128]{2,1,0:T(8,128)(2,1)S(1)} %get-tuple-element.5), kind=kOutput, calls=%fused_computation.7 | convolution fusion | flops 2164391936 | bytes 12058628 | tf_op jit(solution)/shard_map/nc,jcb->jbn/dot_general | solution.py:91
  143.3 1.6 broadcast_in_dim.7
  144.9 10.2 %all-to-all-start = ((f32[4,1,256,512]{3,2,1,0:T(8,128)}), f32[4,1,256,512]{3,2,1,0:T(8,128)S(1)}, u32[]{:S(2)}, u32[]{:S(2)}) async-start(f32[4,1,256,512]{3,2,1,0:T(8,128)} %broadcast_in_dim.7), calls=%async_computation | async-start | bytes 4194304 | tf_op jit(solution)/shard_map/all_to_all | solution.py:14
  155.1 0.0 reduce-scatter.4.cloned.1.call-start
  155.1 0.0 copy-done.2
  155.1 0.0 copy-done.3
  155.1 0.3 fusion.37
  155.4 10.9 %maximum_maximum_fusion = bf16[1,8192,256]{2,1,0:T(8,128)(2,1)} fusion(bf16[1,4096,128]{2,1,0:T(8,128)(2,1)} %copy-done.1, bf16[1,4096,128]{2,1,0:T(8,128)(2,1)S(1)} %fusion.73, bf16[1,4096,128]{2,1,0:T(8,128)(2,1)} %copy-done), kind=kLoop, calls=%fused_computation.1 | loop fusion | flops 16777216 | bytes 7340032 | tf_op jit(solution)/shard_map/vmap()/concatenate | solution.py:51
  166.2 0.0 copy-start.4
  166.2 14.7 %all-to-all-done = f32[4,1,256,512]{3,2,1,0:T(8,128)S(1)} async-done(((f32[4,1,256,512]{3,2,1,0:T(8,128)}), f32[4,1,256,512]{3,2,1,0:T(8,128)S(1)}, u32[]{:S(2)}, u32[]{:S(2)}) %all-to-all-start) | async-done | bytes 2097184 | tf_op jit(solution)/shard_map/all_to_all | solution.py:14
  180.9 0.2 reduce_sum.19
  181.1 4.9 %fusion.27 = f32[128,512]{1,0:T(8,128)S(1)} fusion(f32[1,2,128,512]{3,2,1,0:T(8,128)S(1)} %bitcast.67), kind=kOutput, calls=%fused_computation.35 | convolution fusion | flops 406323200 | bytes 524288 | tf_op jit(solution)/shard_map/...c,ck->...k/dot_general | solution.py:55
  186.0 4.9 %fusion.31 = f32[128,512]{1,0:T(8,128)S(1)} fusion(f32[1,2,128,512]{3,2,1,0:T(8,128)S(1)} %bitcast.68), kind=kOutput, calls=%fused_computation.37 | convolution fusion | flops 406323200 | bytes 524288 | tf_op jit(solution)/shard_map/...c,ck->...k/dot_general | solution.py:55
  190.9 0.0 copy-done.4
  190.9 4.9 %fusion.9 = f32[128,512]{1,0:T(8,128)S(1)} fusion(f32[128,512]{1,0:T(8,128)S(1)} %fusion.37, f32[128,512]{1,0:T(8,128)S(1)} %fusion.27, f32[1,2,128,512]{3,2,1,0:T(8,128)S(1)} %bitcast.69, bf16[1,2,128,512]{3,2,1,0:T(8,128)(2,1)S(1)} %copy-done.4), kind=kOutput, calls=%fused_computation.15 | convolution fusion | flops 406650880 | bytes 1179648 | tf_op jit(solution)/shard_map/...c,ck->...k/dot_general | solution.py:55
  195.7 5.0 %fusion.25 = f32[128,512]{1,0:T(8,128)S(1)} fusion(f32[128,512]{1,0:T(8,128)S(1)} %fusion.9), kind=kOutput, calls=%fused_computation.34 | convolution fusion | flops 406323200 | bytes 524288 | tf_op jit(solution)/shard_map/...c,ck->...k/dot_general | solution.py:55
  200.8 4.9 %fusion.12 = f32[128,512]{1,0:T(8,128)S(1)} fusion(f32[128,512]{1,0:T(8,128)S(1)} %fusion.37, f32[128,512]{1,0:T(8,128)S(1)} %fusion.31, f32[1,2,128,512]{3,2,1,0:T(8,128)S(1)} %bitcast.70, bf16[1,2,128,512]{3,2,1,0:T(8,128)(2,1)S(1)} %copy-done.4), kind=kOutput, calls=%fused_computation.19 | convolution fusion | flops 406650880 | bytes 1179648 | tf_op jit(solution)/shard_map/...c,ck->...k/dot_general | solution.py:55
  205.7 4.9 %fusion.29 = f32[128,512]{1,0:T(8,128)S(1)} fusion(f32[128,512]{1,0:T(8,128)S(1)} %fusion.12), kind=kOutput, calls=%fused_computation.36 | convolution fusion | flops 406323200 | bytes 524288 | tf_op jit(solution)/shard_map/...c,ck->...k/dot_general | solution.py:55
  210.5 4.7 fusion.15
  215.3 4.9 %fusion.16 = bf16[1,1,128,512]{3,2,1,0:T(8,128)(2,1)S(1)} fusion(f32[128,512]{1,0:T(8,128)S(1)} %fusion.29, f32[128,512]{1,0:T(8,128)S(1)} %fusion.9), kind=kOutput, calls=%fused_computation.23 | convolution fusion | flops 406519808 | bytes 655360 | tf_op jit(solution)/shard_map/...c,ck->...k/dot_general | solution.py:55
  220.3 0.1 copy.16
  220.4 4.6 convolution_bitcast_fusion
  225.0 6.2 %copy.17 = f32[4,4,4,8,2,4096]{5,3,4,2,1,0:T(8,128)} copy(f32[4,4,4,8,2,4096]{5,3,4,1,2,0:T(8,128)S(1)} %convolution_bitcast_fusion) | data formatting | bytes 33554432 | tf_op jit(solution)/shard_map/transpose | solution.py:24
  231.2 0.0 reduce-scatter.4.cloned.1.call-update
  231.2 0.0 reduce-scatter.6.cloned.1.call-start
  231.2 148.6 %reduce-scatter.4.cloned.1.call-done = f32[16,8,2,4096]{3,1,2,0:T(8,128)} async-done(((f32[64,8,2,4096]{3,1,2,0:T(8,128)}), f32[16,8,2,4096]{3,1,2,0:T(8,128)}) %reduce-scatter.4.cloned.1.call-update) | async-done | bytes 4194320 | tf_op jit(solution)/shard_map/reduce_scatter | solution.py:27
  379.8 0.0 reduce-scatter.6.cloned.1.call-update
  379.9 0.0 reduce-scatter.8.cloned.1.call-start
  379.9 52.9 %reduce-scatter.6.cloned.1.call-done = f32[4,8,2,4096]{3,1,2,0:T(8,128)} async-done(((f32[16,8,2,4096]{3,1,2,0:T(8,128)}), f32[4,8,2,4096]{3,1,2,0:T(8,128)}) %reduce-scatter.6.cloned.1.call-update) | async-done | bytes 1048592 | tf_op jit(solution)/shard_map/reduce_scatter | solution.py:27
  432.8 0.0 reduce-scatter.8.cloned.1.call-update
  432.8 36.3 %reduce-scatter.8.cloned.1.call-done = f32[1,8,2,4096]{3,1,2,0:T(8,128)} async-done(((f32[4,8,2,4096]{3,1,2,0:T(8,128)}), f32[1,8,2,4096]{3,1,2,0:T(8,128)}) %reduce-scatter.8.cloned.1.call-update) | async-done | bytes 262160 | tf_op jit(solution)/shard_map/reduce_scatter | solution.py:27
  469.0 1.9 copy.18
  (1 shorter events, 0.0 us)
Async XLA Ops:
  6.5 114.2 %all-gather.2.cloned.1.call-start = ((), (), s32[]{:S(2)}) async-start(), calls=%async_computation.4 | async-start | bytes 8519680 | tf_op jit(solution)/shard_map/all_gather | solution.py:89
  12.3 124.7 %copy-start = (bf16[1,4096,128]{2,1,0:T(8,128)(2,1)}, bf16[1,4096,128]{2,1,0:T(8,128)(2,1)S(1)}, u32[]{:S(2)}) copy-start(bf16[1,4096,128]{2,1,0:T(8,128)(2,1)S(1)} %get-tuple-element.5) | copy-start | bytes 3145732
  12.3 124.7 %copy-start.1 = (bf16[1,4096,128]{2,1,0:T(8,128)(2,1)}, bf16[1,4096,128]{2,1,0:T(8,128)(2,1)S(1)}, u32[]{:S(2)}) copy-start(bf16[1,4096,128]{2,1,0:T(8,128)(2,1)S(1)} %get-tuple-element.6) | copy-start | bytes 3145732
  137.0 18.1 %copy-start.2 = (s32[32,512]{1,0:T(8,128)S(1)}, s32[32,512]{1,0:T(8,128)}, u32[]{:S(2)}) copy-start(s32[32,512]{1,0:T(8,128)} %param.11) | copy-start | bytes 196612
  137.0 18.1 %copy-start.3 = (s32[1,128]{1,0:T(1,128)S(1)}, s32[1,128]{1,0:T(1,128)}, u32[]{:S(2)}) copy-start(s32[1,128]{1,0:T(1,128)} %param.10) | copy-start | bytes 1540
  144.9 36.0 %all-to-all-start = ((f32[4,1,256,512]{3,2,1,0:T(8,128)}), f32[4,1,256,512]{3,2,1,0:T(8,128)S(1)}, u32[]{:S(2)}, u32[]{:S(2)}) async-start(f32[4,1,256,512]{3,2,1,0:T(8,128)} %broadcast_in_dim.7), calls=%async_computation | async-start | bytes 4194304 | tf_op jit(solution)/shard_map/all_to_all | solution.py:14
  155.1 224.8 %reduce-scatter.4.cloned.1.call-start = ((), (), s32[]{:S(2)}) async-start(), calls=%async_computation.5 | async-start | bytes 20971520 | tf_op jit(solution)/shard_map/reduce_scatter | solution.py:27
  166.2 24.6 %copy-start.4 = (bf16[1,2,128,512]{3,2,1,0:T(8,128)(2,1)S(1)}, bf16[1,2,128,512]{3,2,1,0:T(8,128)(2,1)}, u32[]{:S(2)}) copy-start(bf16[1,2,128,512]{3,2,1,0:T(8,128)(2,1)} %param.8) | copy-start | bytes 786436
  231.2 201.6 %reduce-scatter.6.cloned.1.call-start = ((), (), s32[]{:S(2)}) async-start(), calls=%async_computation.6 | async-start | bytes 5242880 | tf_op jit(solution)/shard_map/reduce_scatter | solution.py:27
  379.9 89.2 %reduce-scatter.8.cloned.1.call-start = ((), (), s32[]{:S(2)}) async-start(), calls=%async_computation.7 | async-start | bytes 1310720 | tf_op jit(solution)/shard_map/reduce_scatter | solution.py:27
Sparse Core Ops, SparseCore 0:
  10.6 110.0 all-gather.1
  231.3 148.4 reduce-scatter.3
  382.4 50.3 reduce-scatter.5
  435.2 33.8 reduce-scatter.7
where the time goes:
time: 487 us; the launch traced here: 478 us
  waiting for transfers between devices  362 us (74%)
  matrix products  50.2 us (10%)
  local copies, waits for them, and re-layouts  27.7 us (6%)
  between operations  14.2 us (3%)
  other arithmetic  13.8 us (3%)
  starting transfers between devices  10.3 us (2%)
    reduce_scatter x3, waiting for transfers between devices, own_block(): tiles = lax.psum_scatter(tiles, axes[k], scatter_dimension=0, tiled=True)  238 us
    all_gather x1, waiting for transfers between devices, body(): sky_piece = lax.all_gather(sky, FREQ, axis=1, tiled=True)  108 us
    dot_general x8, matrix products, transform(): jnp.einsum('...c,ck->...k', values, table, precision=lax.Precision.HIGHEST)  39 us
    unnamed x11, local copies, waits for them, and re-layouts  16.2 us
    all_to_all x1, waiting for transfers between devices, sent_to_all(): return lax.all_to_all(copies, axis, split_axis=0, concat_axis=0, tiled=True)  14.7 us
    concatenate x1, other arithmetic, real_form(): return jnp.concatenate([upper_half, lower_half], axis=0)  10.9 us
    all_to_all x1, starting transfers between devices, sent_to_all(): return lax.all_to_all(copies, axis, split_axis=0, concat_axis=0, tiled=True)  10.2 us
  transfers between devices with their start and end apart: 5, of which 5 were waited for; matrix products, arithmetic and copies ran while one was open for 3% of the time, Pallas kernels for 0%

commit v1 on v0

v1 whole, which is shorter than its diff:
```python
import functools
import math

import jax
import jax.numpy as jnp
import numpy as np
from jax import lax
from jax.experimental import pallas as pl
from jax.experimental.pallas import tpu as pltpu
from jax.sharding import Mesh
from jax.sharding import PartitionSpec as P

FREQ = ("freq_0", "freq_1", "freq_2")
AXES = ("tile",) + FREQ
RING = 4
ROWS = 16
GATHER_PLANES = (0, 1, 3, 2)
REDUCE_PLANES = (2, 1, 3, 0)


def at(dx, dy):
    return (dx % RING) * RING + dy % RING


def forward_class(dz, other):
    return 1 if (dz + other) % 2 == 0 else -1


def gather_keys():
    keys = [(dz, 0, "F") for dz in range(1, RING)]
    for dz in range(RING):
        for d in range(1, RING):
            keys += [(dz, at(d, 0), "F"), (dz, at(0, d), "F")]
        for dx in range(1, RING):
            for dy in range(1, RING):
                keys += [(dz, at(dx, dy), "A"), (dz, at(dx, dy), "B")]
    return {key: n for n, key in enumerate(keys)}


GATHER = gather_keys()


def reduce_slots():
    halves, fulls = [], []
    for dz in range(RING):
        for d in range(1, RING):
            for came in (1, -1):
                halves.append((dz, at(d, 0), "A", "y", came))
                halves.append((dz, at(0, d), "B", "x", came))
            side = forward_class(dz, d)
            halves.append((dz, at(d, -side), "A", "y", side))
            halves.append((dz, at(-side, d), "B", "x", side))
        side = forward_class(dz, 0)
        fulls.append((dz, at(-side, 0), "F", "x", side))
        fulls.append((dz, at(0, -side), "F", "y", side))
        for axis in "xy":
            for came in (1, -1):
                fulls.append((dz, 0, "F", axis, came))
    return {k: n for n, k in enumerate(halves)}, {k: n for n, k in enumerate(fulls)}


HALVES, FULLS = reduce_slots()


def kernel(
    bt_ref, sky_ref, ker_ref, data_ref, bins_ref, wedge_ref, thi_ref, tlo_ref, out_ref,
    buf, kc, acc, vp, t1r, hs, hr, vis, spec, vhi, vlo, mask, dat, u, g,
    rs_h, rs_f, zs, zr,
    local_sem, send_sem, ag_sem, t_send, t_recv, rh_sem, rf_sem, z_send, z_recv,
):
    tile = lax.axis_index("tile")
    y = lax.axis_index("freq_0")
    z = lax.axis_index("freq_1")
    x = lax.axis_index("freq_2")
    cells = sky_ref.shape[1]
    half = cells // 2
    chans, base = vis.shape[1], vis.shape[2]
    per = chans // RING**3
    core = lax.rem(tile, 2)
    mate = tile + 1 - 2 * core

    def near(axis, step):
        if axis == "x":
            return (tile, y, z, lax.rem(x + step + RING, RING))
        if axis == "y":
            return (tile, lax.rem(y + step + RING, RING), z, x)
        return (tile, y, lax.rem(z + step + RING, RING), x)

    over = lax.rem(tile + 2, 4)
    cross = lax.rem(mate + 2, 4)
    peers = [near("x", 1), near("x", -1), near("y", 1), near("y", -1)]
    peers += [near("z", d) for d in (1, 2, 3)]
    peers += [(t, y, z, x) for t in (mate, over, cross)]

    load_sky = pltpu.make_async_copy(sky_ref, buf.at[0, 0], local_sem.at[0])
    load_r = pltpu.make_async_copy(ker_ref.at[0], kc.at[:, 0:base], local_sem.at[1])
    load_i = pltpu.make_async_copy(ker_ref.at[1], kc.at[:, base : 2 * base], local_sem.at[2])
    load_sky.start()
    load_r.start()
    load_i.start()
    barrier = pltpu.get_barrier_semaphore()
    for peer in peers:
        pl.semaphore_signal(barrier, inc=1, device_id=peer, device_id_type=pl.DeviceIdType.MESH)
    pl.semaphore_wait(barrier, len(peers))

    def part_of(ref, dz, cell, part):
        if part == "F":
            return ref.at[dz, cell]
        lo = 0 if part == "A" else half
        return ref.at[dz, cell, :, lo : lo + half]

    def remote(src, dst, send, recv, peer):
        return pltpu.make_async_remote_copy(
            src_ref=src, dst_ref=dst, send_sem=send, recv_sem=recv,
            device_id=peer, device_id_type=pl.DeviceIdType.MESH,
        )

    weight = bt_ref[0, tile].astype(jnp.float32)

    sent = []

    def gather_send(dz, dx, dy, part, axis, step):
        if axis == "z":
            new = ((dz - step) % RING, 0)
        else:
            new = (dz, at(dx - step, dy) if axis == "x" else at(dx, dy - step))
        copy = remote(
            part_of(buf, dz, at(dx, dy), part),
            part_of(buf, *new, part),
            send_sem.at[len(sent)],
            ag_sem.at[GATHER[(*new, part)]],
            near(axis, step),
        )
        copy.start()
        sent.append(copy)

    def gather_wait(dz, dx, dy, part):
        ref = part_of(buf, dz, at(dx, dy), part)
        remote(ref, ref, send_sem.at[0], ag_sem.at[GATHER[(dz, at(dx, dy), part)]],
               near("x", 1)).wait_recv()

    def g1(dz):
        if dz:
            gather_wait(dz, 0, 0, "F")
        for axis in "xy":
            for step in (1, -1):
                gather_send(dz, 0, 0, "F", axis, step)

    def g2(dz):
        side = forward_class(dz, 0)
        for d in (-side, side):
            for axis, turn, part in (("x", "y", "A"), ("y", "x", "B")):
                dx, dy = (d, 0) if axis == "x" else (0, d)
                gather_wait(dz, dx, dy, "F")
                if d == -side:
                    gather_send(dz, dx, dy, "F", axis, side)
                for step in (1, -1):
                    gather_send(dz, dx, dy, part, turn, step)

    def g3(dz):
        for turn, part, dx, dy in (("y", "A", 2, 0), ("x", "B", 0, 2)):
            gather_wait(dz, dx, dy, "F")
            for step in (1, -1):
                gather_send(dz, dx, dy, part, turn, step)

    def g4(dz):
        for d in (1, 3, 2):
            side = forward_class(dz, d)
            for far in (-side, side):
                gather_wait(dz, d, far, "A")
                if far == -side:
                    gather_send(dz, d, far, "A", "y", side)
                gather_wait(dz, far, d, "B")
                if far == -side:
                    gather_send(dz, far, d, "B", "x", side)

    def g5(dz):
        for d in (1, 3, 2):
            gather_wait(dz, d, 2, "A")
            gather_wait(dz, 2, d, "B")

    depth = 512
    deep = cells // depth

    def forward(dz):
        acc[...] = jnp.zeros_like(acc)

        @pl.loop(0, deep)
        def _(k):
            lanes = pl.ds(pl.multiple_of(k * depth, depth), depth)
            rows = buf[dz, :, :, lanes].reshape(RING * RING * ROWS, depth)
            acc[...] += jnp.dot(rows, kc[lanes, :], preferred_element_type=jnp.float32)

        out = acc[...].reshape(RING * RING, 2, per, 2 * base)
        real = out[:, 0, :, :base] - out[:, 1, :, base:]
        imag = out[:, 1, :, :base] + out[:, 0, :, base:]
        vp[dz, 0] = (real * weight).reshape(RING * RING * per, base)
        vp[dz, 1] = (imag * weight).reshape(RING * RING * per, base)

    def t1(dz):
        return remote(vp.at[dz, 1 - core], t1r.at[dz], t_send.at[dz, 0], t_recv.at[dz, 0],
                      (mate, y, z, x))

    def t2(dz):
        return [
            remote(hs.at[dz], hr.at[dz, n], t_send.at[dz, n + 1], t_recv.at[dz, n + 1],
                   (t, y, z, x))
            for n, t in enumerate((mate, over, cross))
        ]

    def tile_first(dz):
        forward(dz)
        t1(dz).start()

    def tile_second(dz):
        t1(dz).wait_recv()
        hs[dz] = vp[dz, core] + t1r[dz]
        for copy in t2(dz):
            copy.start()

    def row_of(dz, cell):
        sx = lax.rem(x + cell // RING, RING)
        sy = lax.rem(y + cell % RING, RING)
        sz = lax.rem(z + dz, RING)
        return pl.multiple_of((sy * RING * RING + sz * RING + sx) * per, per)

    def tile_third(dz):
        for copy in t2(dz):
            copy.wait_recv()
        for cell in range(RING * RING):
            mine = pl.ds(cell * per, per)
            rows = pl.ds(row_of(dz, cell), per)
            vis[core, rows, :] = hs[dz, mine, :] + hr[dz, 1, mine, :]
            vis[1 - core, rows, :] = hr[dz, 0, mine, :] + hr[dz, 2, mine, :]

    def prepare():
        levels = lax.broadcasted_iota(jnp.int32, (wedge_ref.shape[0], base), 0)
        hot = (levels == bins_ref[...]).astype(jnp.bfloat16)
        keep = wedge_ref[...].astype(jnp.float32).T.astype(jnp.bfloat16)
        mask[...] = jnp.dot(keep, hot, preferred_element_type=jnp.float32)
        for plane in range(2):
            dat[plane] = data_ref[plane].astype(jnp.float32).T

    load_sky.wait()
    for step in (1, 3, 2):
        gather_send(0, 0, 0, "F", "z", step)
    p = GATHER_PLANES
    g1(p[0])
    prepare()
    g1(p[1])
    g2(p[0])
    g3(p[0])
    load_r.wait()
    load_i.wait()
    g1(p[2])
    g2(p[1])
    g4(p[0])
    g3(p[1])
    g1(p[3])
    g2(p[2])
    g5(p[0])
    tile_first(p[0])
    g4(p[1])
    g3(p[2])
    g2(p[3])
    tile_second(p[0])
    g5(p[1])
    tile_first(p[1])
    g4(p[2])
    g3(p[3])
    tile_second(p[1])
    tile_third(p[0])
    g5(p[2])
    tile_first(p[2])
    g4(p[3])
    tile_second(p[2])
    tile_third(p[1])
    g5(p[3])
    tile_first(p[3])
    tile_third(p[2])
    tile_second(p[3])
    for copy in sent:
        copy.wait_send()
    tile_third(p[3])
    for dz in range(RING):
        for copy in (t1(dz), *t2(dz)):
            copy.wait_send()

    norm = 1.0 / math.sqrt(chans)
    block = 256

    def transform():
        for plane in range(2):
            lanes = slice(plane * base, (plane + 1) * base)
            whole = vis[plane]
            vhi[:, lanes] = whole.astype(jnp.bfloat16)
            vlo[:, lanes] = (whole - vhi[:, lanes].astype(jnp.float32)).astype(jnp.bfloat16)

        @pl.loop(0, 2 * chans // block)
        def _(n):
            rows = pl.ds(pl.multiple_of(n * block, block), block)
            spec[rows, :] = (
                jnp.dot(thi_ref[rows, :], vhi[...], preferred_element_type=jnp.float32)
                + jnp.dot(thi_ref[rows, :], vlo[...], preferred_element_type=jnp.float32)
                + jnp.dot(tlo_ref[rows, :], vhi[...], preferred_element_type=jnp.float32)
            )

    cos_rows, sin_rows = slice(0, chans), slice(chans, 2 * chans)
    lane_r, lane_i = slice(0, base), slice(base, 2 * base)
    transform()
    vis[0] = mask[...] * (
        (spec[cos_rows, lane_r] + spec[sin_rows, lane_i]) * norm - dat[0]
    )
    vis[1] = mask[...] * (
        (spec[cos_rows, lane_i] - spec[sin_rows, lane_r]) * norm - dat[1]
    )
    transform()
    vis[0] = (spec[cos_rows, lane_r] - spec[sin_rows, lane_i]) * (norm * weight)
    vis[1] = (spec[cos_rows, lane_i] + spec[sin_rows, lane_r]) * (norm * weight)
    for dz in range(RING):
        for cell in range(RING * RING):
            rows = pl.ds(row_of(dz, cell), per)
            ur, ui = vis[0, rows, :], vis[1, rows, :]
            top = jnp.concatenate([ur, ui], axis=1)
            low = jnp.concatenate([ui, -ur], axis=1)
            u[dz, cell] = jnp.concatenate([top, low], axis=0).astype(jnp.bfloat16)

    def backward(dz):
        rows = u[dz].reshape(RING * RING * ROWS, 2 * base)

        @pl.loop(0, deep)
        def _(k):
            lanes = pl.ds(pl.multiple_of(k * depth, depth), depth)
            part = lax.dot_general(
                rows, kc[lanes, :], (((1,), (1,)), ((), ())),
                preferred_element_type=jnp.float32,
            )
            g[dz, :, :, lanes] = part.reshape(RING * RING, ROWS, depth)

    back_sent = []

    def slot(dz, cell, part, axis, came):
        key = (dz, cell, part, axis, came)
        if part == "F":
            return rs_f.at[FULLS[key]], rf_sem.at[FULLS[key]]
        return rs_h.at[HALVES[key]], rh_sem.at[HALVES[key]]

    def reduce_send(dz, dx, dy, part, axis, step):
        new = at(dx - step, dy) if axis == "x" else at(dx, dy - step)
        dst, sem = slot(dz, new, part, axis, -step)
        copy = remote(
            part_of(buf, dz, at(dx, dy), part), dst, send_sem.at[len(back_sent)], sem,
            near(axis, step),
        )
        copy.start()
        back_sent.append(copy)

    def arrived(dz, dx, dy, part, axis, came):
        ref, sem = slot(dz, at(dx, dy), part, axis, came)
        remote(ref, ref, send_sem.at[0], sem, near("x", 1)).wait_recv()
        return ref, part

    width = 1024

    def total(dst, dz, dx, dy, part, terms):
        cell = at(dx, dy)
        start = half if part == "B" else 0
        stop = half if part == "A" else cells

        def step_of(n):
            lanes = pl.ds(pl.multiple_of(start + n * width, width), width)
            value = g[dz, cell, :, lanes]
            for ref, kind in terms:
                shift = half if kind == "B" else 0
                own = pl.ds(pl.multiple_of(start - shift + n * width, width), width)
                value = value + ref[:, own].astype(jnp.float32)
            dst[:, lanes] = value.astype(dst.dtype)

        pl.loop(0, (stop - start) // width)(step_of)

    def r1(dz):
        backward(dz)
        for d in (2, 1, 3):
            side = forward_class(dz, d)
            total(buf.at[dz, at(d, 2)], dz, d, 2, "A", [])
            reduce_send(dz, d, 2, "A", "y", -side)
            total(buf.at[dz, at(2, d)], dz, 2, d, "B", [])
            reduce_send(dz, 2, d, "B", "x", -side)
            total(buf.at[dz, at(d, side)], dz, d, side, "A", [])
            reduce_send(dz, d, side, "A", "y", side)
            total(buf.at[dz, at(side, d)], dz, side, d, "B", [])
            reduce_send(dz, side, d, "B", "x", side)

    def r2(dz):
        for d in (2, 1, 3):
            side = forward_class(dz, d)
            got = arrived(dz, d, -side, "A", "y", side)
            total(buf.at[dz, at(d, -side)], dz, d, -side, "A", [got])
            reduce_send(dz, d, -side, "A", "y", -side)
            got = arrived(dz, -side, d, "B", "x", side)
            total(buf.at[dz, at(-side, d)], dz, -side, d, "B", [got])
            reduce_send(dz, -side, d, "B", "x", -side)

    def on_axis(dz, axis, d, fulls):
        dx, dy = (d, 0) if axis == "x" else (0, d)
        turn, part, rest = ("y", "A", "B") if axis == "x" else ("x", "B", "A")
        got = [arrived(dz, dx, dy, part, turn, came) for came in (1, -1)]
        dst = buf.at[dz, at(dx, dy)]
        total(dst, dz, dx, dy, part, got + fulls)
        total(dst, dz, dx, dy, rest, fulls)

    def r3(dz):
        side = forward_class(dz, 0)
        for axis in "xy":
            dx, dy = (2, 0) if axis == "x" else (0, 2)
            on_axis(dz, axis, 2, [])
            reduce_send(dz, dx, dy, "F", axis, -side)

    def r4(dz):
        side = forward_class(dz, 0)
        for d in (side, -side):
            for axis in "xy":
                dx, dy = (d, 0) if axis == "x" else (0, d)
                fulls = [arrived(dz, dx, dy, "F", axis, side)] if d == -side else []
                on_axis(dz, axis, d, fulls)
                reduce_send(dz, dx, dy, "F", axis, d)

    def z_copy(dz):
        return remote(zs.at[dz - 1], zr.at[dz - 1], z_send.at[dz - 1], z_recv.at[dz - 1],
                      near("z", dz))

    def r5(dz):
        got = [arrived(dz, 0, 0, "F", axis, came) for axis in "xy" for came in (1, -1)]
        if dz:
            total(zs.at[dz - 1], dz, 0, 0, "F", got)
            z_copy(dz).start()
        else:
            for n in (1, 2, 3):
                z_copy(n).wait_recv()
            got += [(zr.at[n], "F") for n in range(RING - 1)]
            total(out_ref, 0, 0, 0, "F", got)

    p = REDUCE_PLANES
    r1(p[0])
    r1(p[1])
    r2(p[0])
    r3(p[0])
    r1(p[2])
    r2(p[1])
    r4(p[0])
    r3(p[1])
    r1(p[3])
    r2(p[2])
    r5(p[0])
    r4(p[1])
    r3(p[2])
    r2(p[3])
    r5(p[1])
    r4(p[2])
    r3(p[3])
    r5(p[2])
    r4(p[3])
    r5(p[3])
    for copy in back_sent:
        copy.wait_send()
    for n in (1, 2, 3):
        z_copy(n).wait_send()


def delay_tables(length):
    indices = np.arange(length, dtype=np.int64)
    angle = (indices[:, None] * indices[None, :] % length) * (2.0 * np.pi / length)
    table = np.concatenate([np.cos(angle), np.sin(angle)], axis=0).astype(np.float32)
    high = table.astype(jnp.bfloat16)
    low = (table - high.astype(np.float32)).astype(jnp.bfloat16)
    return high, low


def body(sky, ker, data, block_tiles, length_bin, wedge_keep):
    per, cells = sky.shape[1], sky.shape[3]
    chans, base = data.shape[3], data.shape[2]
    shard = jnp.transpose(sky[0], (1, 0, 2)).reshape(2 * per, cells)
    high, low = delay_tables(chans)
    full = RING * RING
    vmem = pl.BlockSpec(memory_space=pltpu.VMEM)
    hbm = pl.BlockSpec(memory_space=pl.ANY)
    f32, bf16 = jnp.float32, jnp.bfloat16
    sends = 100
    out = pl.pallas_call(
        kernel,
        out_shape=jax.ShapeDtypeStruct((2 * per, cells), f32),
        in_specs=[pl.BlockSpec(memory_space=pltpu.SMEM), hbm, hbm, vmem, vmem, vmem, vmem, vmem],
        out_specs=vmem,
        scratch_shapes=[
            pltpu.VMEM((RING, full, ROWS, cells), bf16),
            pltpu.VMEM((cells, 2 * base), bf16),
            pltpu.VMEM((full * ROWS, 2 * base), f32),
            pltpu.VMEM((RING, 2, full * per, base), f32),
            pltpu.VMEM((RING, full * per, base), f32),
            pltpu.VMEM((RING, full * per, base), f32),
            pltpu.VMEM((RING, 3, full * per, base), f32),
            pltpu.VMEM((2, chans, base), f32),
            pltpu.VMEM((2 * chans, 2 * base), f32),
            pltpu.VMEM((chans, 2 * base), bf16),
            pltpu.VMEM((chans, 2 * base), bf16),
            pltpu.VMEM((chans, base), f32),
            pltpu.VMEM((2, chans, base), f32),
            pltpu.VMEM((RING, full, ROWS, 2 * base), bf16),
            pltpu.VMEM((RING, full, ROWS, cells), f32),
            pltpu.VMEM((len(HALVES), ROWS, cells // 2), bf16),
            pltpu.VMEM((len(FULLS), ROWS, cells), bf16),
            pltpu.VMEM((RING - 1, ROWS, cells), f32),
            pltpu.VMEM((RING - 1, ROWS, cells), f32),
            pltpu.SemaphoreType.DMA((3,)),
            pltpu.SemaphoreType.DMA((sends,)),
            pltpu.SemaphoreType.DMA((len(GATHER),)),
            pltpu.SemaphoreType.DMA((RING, 4)),
            pltpu.SemaphoreType.DMA((RING, 4)),
            pltpu.SemaphoreType.DMA((len(HALVES),)),
            pltpu.SemaphoreType.DMA((len(FULLS),)),
            pltpu.SemaphoreType.DMA((RING - 1,)),
            pltpu.SemaphoreType.DMA((RING - 1,)),
        ],
        compiler_params=pltpu.CompilerParams(
            collective_id=0, has_side_effects=True, vmem_limit_bytes=60 * 2**20
        ),
    )(block_tiles, shard, ker[0, 0], data[0], length_bin, wedge_keep, high, low)
    return jnp.transpose(out.reshape(2, per, cells), (1, 0, 2))[None]


def solution(mesh):
    finer = Mesh(mesh.devices.reshape(mesh.shape["tile"], RING, RING, RING), AXES)
    return jax.shard_map(
        body,
        mesh=finer,
        in_specs=(
            P("tile", FREQ, None, None),
            P("tile", FREQ, None, None, None),
            P(FREQ, None, None, None),
            P(FREQ, None),
            P(FREQ, None),
            P(),
        ),
        out_specs=P("tile", FREQ, None, None),
        check_vma=False,
    )
```

time: 487 us -> 146 us (0.30); the launches traced: 478 us -> 143 us
  waiting for transfers between devices: 362 us -> 0 us
  Pallas kernels: 0 us -> 139 us
  matrix products: 50.2 us -> 0 us
  local copies, waits for them, and re-layouts: 27.7 us -> 3.49 us
  between operations: 14.2 us -> 0.01 us
  other arithmetic: 13.8 us -> 0 us
  starting transfers between devices: 10.3 us -> 0 us
    reduce_scatter x3 -> x0, waiting for transfers between devices: 238 us -> none  [own_block(): tiles = lax.psum_scatter(tiles, axes[k], scatter_dimension=0, tiled=True)]
    pallas_call x0 -> x1, Pallas kernels: none -> 139 us  [body(): pl.pallas_call(kernel, out_shape=jax.ShapeDtypeStruct((2 * per, cells), f...]
    all_gather x1 -> x0, waiting for transfers between devices: 108 us -> none  [body(): sky_piece = lax.all_gather(sky, FREQ, axis=1, tiled=True)]
    dot_general x11 -> x0, matrix products: 50.2 us -> none  [the longest x8 39 us: transform(): jnp.einsum('...c,ck->...k', values, table, precision=lax.Precision.HIGHEST)]
    unnamed x11 -> x0, local copies, waits for them, and re-layouts: 16.2 us -> none
    all_to_all x1 -> x0, waiting for transfers between devices: 14.7 us -> none  [sent_to_all(): return lax.all_to_all(copies, axis, split_axis=0, concat_axis=0, tiled=True)]
    concatenate x1 -> x0, other arithmetic: 10.9 us -> none  [real_form(): return jnp.concatenate([upper_half, lower_half], axis=0)]
    all_to_all x1 -> x0, starting transfers between devices: 10.2 us -> none  [sent_to_all(): return lax.all_to_all(copies, axis, split_axis=0, concat_axis=0, tiled=True)]
  transfers between devices with their start and end apart: 5 -> 0, of which waited for: 5 -> 0; matrix products, arithmetic and copies ran while one was open for 3% -> 0% of each run, Pallas kernels for 0% -> 0%
where the time goes in v1:
time: 146 us; the launch traced here: 143 us
  Pallas kernels  139 us (95%)
  local copies, waits for them, and re-layouts  3.49 us (2%)
    pallas_call x1, Pallas kernels, body(): pl.pallas_call(kernel, out_shape=jax.ShapeDtypeStruct((2 * per, cells), f...  139 us

profile of v1, /device:TPU:8, one launch (start us, length us, event | category | flops | bytes accessed | tf_op | source)
XLA Modules:
  0.0 142.9 jit_solution(15434865490102239609)
XLA Ops:
  0.0 1.6 %copy.14 = bf16[2,8,4096]{2,1,0:T(8,128)(2,1)} copy(bf16[2,8,4096]{2,0,1:T(2,128)(2,1)} %bitcast.18) | data formatting | bytes 262144 | tf_op jit(solution)/shard_map/transpose | solution.py:482
  1.6 139.4 %shard_map.82 = f32[16,4096]{1,0:T(8,128)} custom-call(s32[1,4]{1,0:T(1,128)} %bt_ref.1, bf16[16,4096]{1,0:T(8,128)(2,1)} %bitcast.16, bf16[2,4096,128]{2,1,0:T(8,128)(2,1)} %bitcast.14, bf16[2,128,512]{2,1,0:T(8,128)(2,1)} %bitcast.17, s32[1,128]{1,0:T(1,128)} %bins_ref.1, s32[32,512]{1,0:T(8,128)} %wedge_ref.1, bf16[1024,512]{1,0:T(8,128)(2,1)} %constant.4.clone.thi_ref, ...), custom_call_target="tpu_custom_call" | custom-call | tf_op jit(solution)/shard_map/pallas_call | solution.py:489
  141.1 1.9 %copy.13 = f32[2,8,4096]{2,0,1:T(2,128)} copy(f32[2,8,4096]{2,1,0:T(8,128)} %bitcast.15) | data formatting | bytes 524288 | tf_op jit(solution)/shard_map/reshape | solution.py:528

commit v2 on v0

v2 whole, which is shorter than its diff:
```python
import functools
import math

import jax
import jax.numpy as jnp
import numpy as np
from jax import lax
from jax.experimental import pallas as pl
from jax.experimental.pallas import tpu as pltpu
from jax.sharding import Mesh
from jax.sharding import PartitionSpec as P

FREQ = ("freq_0", "freq_1", "freq_2")
AXES = ("tile",) + FREQ
RING = 4
ROWS = 16
CORNER = 2 * RING + 2
SERVE = (
    0, 9, 12, 36, 3, 23, 48, 6, 40, 47, 22, 24, 16, 17, 41, 51, 60, 43, 84, 57, 96, 35, 46, 29,
    34, 19, 28, 94, 95, 65, 70, 54, 144, 20, 44, 64, 105, 89, 71, 83, 91, 132, 88, 31, 67, 72,
    180, 153, 32, 92, 99, 147, 108, 143, 77, 102, 156, 127, 167, 184, 68, 142, 120, 76, 136, 190,
    191, 119, 176, 112, 161, 137, 113, 150, 160, 116, 166, 175, 79, 185, 168, 124, 130, 140, 82,
    118, 80, 131, 139, 179, 128, 125, 115, 187, 188, 164, 163, 172, 178, 173,
)
ISSUE = (
    9, 48, 144, 12, 96, 3, 36, 23, 6, 47, 16, 22, 46, 40, 24, 41, 17, 35, 84, 60, 51, 57, 20, 44,
    43, 28, 34, 19, 29, 89, 65, 54, 64, 72, 70, 88, 94, 71, 95, 99, 105, 132, 108, 31, 91, 83, 67,
    92, 68, 153, 180, 156, 147, 32, 119, 143, 102, 77, 136, 120, 142, 127, 79, 175, 82, 76, 184,
    190, 191, 167, 176, 80, 128, 137, 113, 150, 185, 161, 118, 112, 140, 116, 168, 160, 166, 124,
    130, 139, 187, 179, 131, 115, 125, 188, 164, 163, 173, 172, 178,
)
RETURN = (
    116, 140, 130, 124, 125, 143, 137, 142, 118, 139, 115, 131, 92, 102, 76, 120, 136, 113, 119,
    128, 77, 188, 112, 164, 67, 88, 91, 68, 82, 65, 79, 172, 175, 127, 161, 99, 132, 108, 163, 80,
    176, 105, 178, 72, 89, 184, 71, 94, 150, 83, 167, 179, 173, 187, 64, 54, 95, 191, 160, 96, 70,
    168, 166, 32, 185, 190, 60, 57, 153, 84, 51, 180, 156, 147, 20, 31, 41, 19, 28, 29, 48, 44,
    22, 47, 144, 34, 35, 43, 6, 17, 24, 16, 23, 46, 40, 12, 3, 9, 36, 0,
)


def at(dx, dy):
    return (dx % RING) * RING + dy % RING


def decoded(code):
    return code // 48, code // 3 % 16, "FAB"[code % 3]


def side_of(dz, other):
    return 1 if (dz + other) % 2 == 0 else -1


def gather_tree():
    kids = {}

    def edge(parent, axis, step, child):
        if not (parent[0] and child[1] == CORNER):
            kids.setdefault(parent, []).append((axis, step, child))

    for step in (1, 3, 2):
        edge((0, 0, "F"), "z", step, (-step % RING, 0, "F"))
        for part in "AB":
            edge((0, CORNER, part), "z", step, (-step % RING, CORNER, part))
    for dz in range(RING):
        for turn, part in (("y", "A"), ("x", "B")):
            axis = "x" if part == "A" else "y"

            def cell(along, across):
                return at(along, across) if axis == "x" else at(across, along)

            side = side_of(dz, 0)
            for step in (1, -1):
                edge((dz, 0, "F"), axis, step, (dz, cell(-step, 0), "F"))
            edge((dz, cell(-side, 0), "F"), axis, side, (dz, cell(2, 0), "F"))
            for d in range(1, RING):
                for step in (1, -1):
                    edge((dz, cell(d, 0), "F"), turn, step, (dz, cell(d, -step), part))
                side_d = side_of(dz, d)
                edge((dz, cell(d, -side_d), part), turn, side_d, (dz, cell(d, 2), part))
    rank = {decoded(code): n for n, code in enumerate(ISSUE)}
    for children in kids.values():
        children.sort(key=lambda child: rank[child[2]])
    return kids


TREE = gather_tree()
PARENT = {child: (axis, step) for kids in TREE.values() for axis, step, child in kids}
SEMAPHORE = {message: n for n, message in enumerate(PARENT)}
HALVES = {m: n for n, m in enumerate(m for m in PARENT if m[2] != "F")}
FULLS = {m: n for n, m in enumerate(m for m in PARENT if m[2] == "F" and m[1])}


def kernel(
    bt_ref, sky_ref, ker_ref, data_ref, bins_ref, wedge_ref, thi_ref, tlo_ref, out_ref,
    buf, kc, acc, vp, t1r, hs, hr, tt, tr, vis, spec, vhi, vlo, mask, dat, u, g,
    rs_h, rs_f, zs, zr, raw, wedge, thi, tlo,
    local_sem, send_sem, ag_sem, rs_sem, t_send, t_recv,
):
    tile = lax.axis_index("tile")
    y = lax.axis_index("freq_0")
    z = lax.axis_index("freq_1")
    x = lax.axis_index("freq_2")
    cells = sky_ref.shape[1]
    half = cells // 2
    chans, base = vis.shape[1], vis.shape[2]
    per = chans // RING**3
    core = lax.rem(tile, 2)
    mate = tile + 1 - 2 * core

    def near(axis, step):
        if axis == "x":
            return (tile, y, z, lax.rem(x + step + RING, RING))
        if axis == "y":
            return (tile, lax.rem(y + step + RING, RING), z, x)
        return (tile, y, lax.rem(z + step + RING, RING), x)

    over = lax.rem(tile + 2, 4)
    peers = [near("x", 1), near("x", -1), near("y", 1), near("y", -1)]
    peers += [near("z", d) for d in (1, 2, 3)]
    peers += [(t, y, z, x) for t in (mate, over)]

    load_sky = pltpu.make_async_copy(sky_ref, buf.at[0, 0], local_sem.at[0])
    load_r = pltpu.make_async_copy(ker_ref.at[0], kc.at[:, 0:base], local_sem.at[1])
    load_i = pltpu.make_async_copy(ker_ref.at[1], kc.at[:, base : 2 * base], local_sem.at[2])
    load_sky.start()
    late = [load_r, load_i]
    for n, (src, dst) in enumerate(
        ((wedge_ref, wedge), (data_ref, raw), (thi_ref, thi), (tlo_ref, tlo))
    ):
        late.append(pltpu.make_async_copy(src, dst, local_sem.at[3 + n]))
    barrier = pltpu.get_barrier_semaphore()
    for peer in peers:
        pl.semaphore_signal(barrier, inc=1, device_id=peer, device_id_type=pl.DeviceIdType.MESH)
    for load in late:
        load.start()
    pl.semaphore_wait(barrier, len(peers))

    def part_of(ref, dz, cell, part):
        if part == "F":
            return ref.at[dz, cell]
        lo = 0 if part == "A" else half
        return ref.at[dz, cell, :, lo : lo + half]

    def remote(src, dst, send, recv, peer):
        return pltpu.make_async_remote_copy(
            src_ref=src, dst_ref=dst, send_sem=send, recv_sem=recv,
            device_id=peer, device_id_type=pl.DeviceIdType.MESH,
        )

    weight = bt_ref[0, tile].astype(jnp.float32)

    sent = []

    def gather_serve(key):
        if key in PARENT:
            ref = part_of(buf, *key)
            remote(ref, ref, send_sem.at[0], ag_sem.at[SEMAPHORE[key]], near("x", 1)).wait_recv()
        for axis, step, child in TREE.get(key, ()):
            copy = remote(
                part_of(buf, *key[:2], child[2]), part_of(buf, *child),
                send_sem.at[SEMAPHORE[child]], ag_sem.at[SEMAPHORE[child]], near(axis, step),
            )
            copy.start()
            sent.append(copy)

    depth = 512
    deep = cells // depth

    def forward(dz):
        acc[...] = jnp.zeros_like(acc)

        @pl.loop(0, deep)
        def _(k):
            lanes = pl.ds(pl.multiple_of(k * depth, depth), depth)
            rows = buf[dz, :, :, lanes].reshape(RING * RING * ROWS, depth)
            acc[...] += jnp.dot(rows, kc[lanes, :], preferred_element_type=jnp.float32)

        out = acc[...].reshape(RING * RING, 2, per, 2 * base)
        real = out[:, 0, :, :base] - out[:, 1, :, base:]
        imag = out[:, 1, :, :base] + out[:, 0, :, base:]
        vp[dz, 0] = (real * weight).reshape(RING * RING * per, base)
        vp[dz, 1] = (imag * weight).reshape(RING * RING * per, base)

    def t1(dz):
        return remote(vp.at[dz, 1 - core], t1r.at[dz], t_send.at[dz, 0], t_recv.at[dz, 0],
                      (mate, y, z, x))

    def t2(dz):
        return remote(hs.at[dz], hr.at[dz], t_send.at[dz, 1], t_recv.at[dz, 1], (over, y, z, x))

    def t3(dz):
        return remote(tt.at[dz], tr.at[dz], t_send.at[dz, 2], t_recv.at[dz, 2], (mate, y, z, x))

    def row_of(dz, cell):
        sx = lax.rem(x + cell // RING, RING)
        sy = lax.rem(y + cell % RING, RING)
        sz = lax.rem(z + dz, RING)
        return pl.multiple_of((sy * RING * RING + sz * RING + sx) * per, per)

    def tile_1(dz):
        forward(dz)
        t1(dz).start()

    def tile_2(dz):
        t1(dz).wait_recv()
        hs[dz] = vp[dz, core] + t1r[dz]
        t2(dz).start()

    def tile_3(dz):
        t2(dz).wait_recv()
        tt[dz] = hs[dz] + hr[dz]
        t3(dz).start()

    def tile_4(dz):
        t3(dz).wait_recv()
        for cell in range(RING * RING):
            mine = pl.ds(cell * per, per)
            rows = pl.ds(row_of(dz, cell), per)
            vis[core, rows, :] = tt[dz, mine, :]
            vis[1 - core, rows, :] = tr[dz, mine, :]

    def prepare():
        for load in late:
            load.wait()
        levels = lax.broadcasted_iota(jnp.int32, (wedge.shape[0], base), 0)
        hot = (levels == bins_ref[...]).astype(jnp.bfloat16)
        keep = wedge[...].astype(jnp.float32).T.astype(jnp.bfloat16)
        mask[...] = jnp.dot(keep, hot, preferred_element_type=jnp.float32)
        for plane in range(2):
            dat[plane] = raw[plane].astype(jnp.float32).T

    load_sky.wait()
    serve = [decoded(code) for code in SERVE]
    final = {key[0]: n for n, key in enumerate(serve)}
    steps = []
    for n, key in enumerate(serve):
        steps.append(functools.partial(gather_serve, key))
        if n == 4:
            steps.append(prepare)
        if final[key[0]] == n:
            steps.append(functools.partial(tile_1, key[0]))
    done = sorted(final, key=final.get)
    lag = {}
    for stage, work in ((1, tile_2), (2, tile_3), (3, tile_4)):
        for rank, dz in enumerate(done):
            lag[(rank + stage, -stage, dz)] = functools.partial(work, dz)
    tail = sorted(lag)
    shift = 0
    for rank, dz in enumerate(done):
        place = next(i for i, s in enumerate(steps) if getattr(s, "func", None) is tile_1
                     and s.args == (dz,))
        now = [lag[k] for k in tail if k[0] == rank and rank < len(done)]
        steps[place + 1 : place + 1] = now
    steps += [lag[k] for k in tail if k[0] >= len(done)]
    for step in steps:
        step()
    for copy in sent:
        copy.wait_send()
    for dz in range(RING):
        for copy in (t1(dz), t2(dz), t3(dz)):
            copy.wait_send()

    norm = 1.0 / math.sqrt(chans)
    block = 256

    def transform():
        for plane in range(2):
            lanes = slice(plane * base, (plane + 1) * base)
            whole = vis[plane]
            vhi[:, lanes] = whole.astype(jnp.bfloat16)
            vlo[:, lanes] = (whole - vhi[:, lanes].astype(jnp.float32)).astype(jnp.bfloat16)

        @pl.loop(0, 2 * chans // block)
        def _(n):
            rows = pl.ds(pl.multiple_of(n * block, block), block)
            spec[rows, :] = (
                jnp.dot(thi[rows, :], vhi[...], preferred_element_type=jnp.float32)
                + jnp.dot(thi[rows, :], vlo[...], preferred_element_type=jnp.float32)
                + jnp.dot(tlo[rows, :], vhi[...], preferred_element_type=jnp.float32)
            )

    cos_rows, sin_rows = slice(0, chans), slice(chans, 2 * chans)
    lane_r, lane_i = slice(0, base), slice(base, 2 * base)
    transform()
    vis[0] = mask[...] * (
        (spec[cos_rows, lane_r] + spec[sin_rows, lane_i]) * norm - dat[0]
    )
    vis[1] = mask[...] * (
        (spec[cos_rows, lane_i] - spec[sin_rows, lane_r]) * norm - dat[1]
    )
    transform()
    vis[0] = (spec[cos_rows, lane_r] - spec[sin_rows, lane_i]) * (norm * weight)
    vis[1] = (spec[cos_rows, lane_i] + spec[sin_rows, lane_r]) * (norm * weight)
    for dz in range(RING):
        for cell in range(RING * RING):
            rows = pl.ds(row_of(dz, cell), per)
            ur, ui = vis[0, rows, :], vis[1, rows, :]
            top = jnp.concatenate([ur, ui], axis=1)
            low = jnp.concatenate([ui, -ur], axis=1)
            u[dz, cell] = jnp.concatenate([top, low], axis=0).astype(jnp.bfloat16)

    def backward(dz, part):
        rows = u[dz].reshape(RING * RING * ROWS, 2 * base)
        first = 0 if part == "A" else deep // 2

        @pl.loop(first, first + deep // 2)
        def _(k):
            lanes = pl.ds(pl.multiple_of(k * depth, depth), depth)
            value = lax.dot_general(
                rows, kc[lanes, :], (((1,), (1,)), ((), ())),
                preferred_element_type=jnp.float32,
            )
            g[dz, :, :, lanes] = value.reshape(RING * RING, ROWS, depth)

    width = 1024

    def total(dst, dz, cell, part, terms):
        start = half if part == "B" else 0
        stop = half if part == "A" else cells

        def step_of(n):
            lanes = pl.ds(pl.multiple_of(start + n * width, width), width)
            value = g[dz, cell, :, lanes]
            for ref, kind in terms:
                shift = half if kind == "B" else 0
                own = pl.ds(pl.multiple_of(start - shift + n * width, width), width)
                value = value + ref[:, own].astype(jnp.float32)
            dst[:, lanes] = value.astype(dst.dtype)

        pl.loop(0, (stop - start) // width)(step_of)

    def returned(key):
        dz, cell, part = key
        axis, step = PARENT[key]
        step = -step % RING if axis == "z" else -step
        if cell == 0 and dz and axis == "z":
            src, dst = zs.at[dz - 1], zr.at[dz - 1]
        else:
            src = part_of(buf, *key)
            dst = rs_f.at[FULLS[key]] if part == "F" else rs_h.at[HALVES[key]]
        n = SEMAPHORE[key]
        return remote(src, dst, send_sem.at[n], rs_sem.at[n], near(axis, step)), src, dst

    ready = set()
    for code in RETURN:
        key = decoded(code)
        dz, cell, part = key
        root = key not in PARENT
        for half_part in "AB" if part == "F" else part:
            if (dz, half_part) not in ready:
                ready.add((dz, half_part))
                backward(dz, half_part)
        got = []
        for _, _, child in TREE.get(key, ()):
            copy, _, dst = returned(child)
            copy.wait_recv()
            got.append((dst, child[2]))
        whole = out_ref if root else zs.at[dz - 1] if cell == 0 else buf.at[dz, cell]
        kinds = {kind for _, kind in got}
        if part == "F" and kinds - {"F"}:
            for half_part in "AB":
                total(whole, dz, cell, half_part, [t for t in got if t[1] in ("F", half_part)])
        else:
            total(whole, dz, cell, part, got)
        if not root:
            returned(key)[0].start()
    for key in PARENT:
        returned(key)[0].wait_send()


def delay_tables(length):
    indices = np.arange(length, dtype=np.int64)
    angle = (indices[:, None] * indices[None, :] % length) * (2.0 * np.pi / length)
    table = np.concatenate([np.cos(angle), np.sin(angle)], axis=0).astype(np.float32)
    high = table.astype(jnp.bfloat16)
    low = (table - high.astype(np.float32)).astype(jnp.bfloat16)
    return high, low


def body(sky, ker, data, block_tiles, length_bin, wedge_keep):
    per, cells = sky.shape[1], sky.shape[3]
    chans, base = data.shape[3], data.shape[2]
    shard = jnp.transpose(sky[0], (1, 0, 2)).reshape(2 * per, cells)
    high, low = delay_tables(chans)
    full = RING * RING
    vmem = pl.BlockSpec(memory_space=pltpu.VMEM)
    hbm = pl.BlockSpec(memory_space=pl.ANY)
    f32, bf16 = jnp.float32, jnp.bfloat16
    out = pl.pallas_call(
        kernel,
        out_shape=jax.ShapeDtypeStruct((2 * per, cells), f32),
        in_specs=[pl.BlockSpec(memory_space=pltpu.SMEM), hbm, hbm, hbm, vmem, hbm, hbm, hbm],
        out_specs=vmem,
        scratch_shapes=[
            pltpu.VMEM((RING, full, ROWS, cells), bf16),
            pltpu.VMEM((cells, 2 * base), bf16),
            pltpu.VMEM((full * ROWS, 2 * base), f32),
            pltpu.VMEM((RING, 2, full * per, base), f32),
            pltpu.VMEM((RING, full * per, base), f32),
            pltpu.VMEM((RING, full * per, base), f32),
            pltpu.VMEM((RING, full * per, base), f32),
            pltpu.VMEM((RING, full * per, base), f32),
            pltpu.VMEM((RING, full * per, base), f32),
            pltpu.VMEM((2, chans, base), f32),
            pltpu.VMEM((2 * chans, 2 * base), f32),
            pltpu.VMEM((chans, 2 * base), bf16),
            pltpu.VMEM((chans, 2 * base), bf16),
            pltpu.VMEM((chans, base), f32),
            pltpu.VMEM((2, chans, base), f32),
            pltpu.VMEM((RING, full, ROWS, 2 * base), bf16),
            pltpu.VMEM((RING, full, ROWS, cells), f32),
            pltpu.VMEM((len(HALVES), ROWS, cells // 2), bf16),
            pltpu.VMEM((len(FULLS), ROWS, cells), bf16),
            pltpu.VMEM((RING - 1, ROWS, cells), f32),
            pltpu.VMEM((RING - 1, ROWS, cells), f32),
            pltpu.VMEM((2, base, chans), bf16),
            pltpu.VMEM(wedge_keep.shape, jnp.int32),
            pltpu.VMEM((2 * chans, chans), bf16),
            pltpu.VMEM((2 * chans, chans), bf16),
            pltpu.SemaphoreType.DMA((7,)),
            pltpu.SemaphoreType.DMA((len(PARENT),)),
            pltpu.SemaphoreType.DMA((len(PARENT),)),
            pltpu.SemaphoreType.DMA((len(PARENT),)),
            pltpu.SemaphoreType.DMA((RING, 3)),
            pltpu.SemaphoreType.DMA((RING, 3)),
        ],
        compiler_params=pltpu.CompilerParams(
            collective_id=0, has_side_effects=True, vmem_limit_bytes=60 * 2**20
        ),
    )(block_tiles, shard, ker[0, 0], data[0], length_bin, wedge_keep, high, low)
    return jnp.transpose(out.reshape(2, per, cells), (1, 0, 2))[None]


def solution(mesh):
    finer = Mesh(mesh.devices.reshape(mesh.shape["tile"], RING, RING, RING), AXES)
    return jax.shard_map(
        body,
        mesh=finer,
        in_specs=(
            P("tile", FREQ, None, None),
            P("tile", FREQ, None, None, None),
            P(FREQ, None, None, None),
            P(FREQ, None),
            P(FREQ, None),
            P(),
        ),
        out_specs=P("tile", FREQ, None, None),
        check_vma=False,
    )
```

time: 487 us -> 130 us (0.27); the launches traced: 478 us -> 129 us
  waiting for transfers between devices: 362 us -> 0 us
  Pallas kernels: 0 us -> 125 us
  matrix products: 50.2 us -> 0 us
  local copies, waits for them, and re-layouts: 27.7 us -> 3.49 us
  between operations: 14.2 us -> 0.01 us
  other arithmetic: 13.8 us -> 0 us
  starting transfers between devices: 10.3 us -> 0 us
    reduce_scatter x3 -> x0, waiting for transfers between devices: 238 us -> none  [own_block(): tiles = lax.psum_scatter(tiles, axes[k], scatter_dimension=0, tiled=True)]
    pallas_call x0 -> x1, Pallas kernels: none -> 125 us  [body(): pl.pallas_call(kernel, out_shape=jax.ShapeDtypeStruct((2 * per, cells), f...]
    all_gather x1 -> x0, waiting for transfers between devices: 108 us -> none  [body(): sky_piece = lax.all_gather(sky, FREQ, axis=1, tiled=True)]
    dot_general x11 -> x0, matrix products: 50.2 us -> none  [the longest x8 39 us: transform(): jnp.einsum('...c,ck->...k', values, table, precision=lax.Precision.HIGHEST)]
    unnamed x11 -> x0, local copies, waits for them, and re-layouts: 16.2 us -> none
    all_to_all x1 -> x0, waiting for transfers between devices: 14.7 us -> none  [sent_to_all(): return lax.all_to_all(copies, axis, split_axis=0, concat_axis=0, tiled=True)]
    concatenate x1 -> x0, other arithmetic: 10.9 us -> none  [real_form(): return jnp.concatenate([upper_half, lower_half], axis=0)]
    all_to_all x1 -> x0, starting transfers between devices: 10.2 us -> none  [sent_to_all(): return lax.all_to_all(copies, axis, split_axis=0, concat_axis=0, tiled=True)]
  transfers between devices with their start and end apart: 5 -> 0, of which waited for: 5 -> 0; matrix products, arithmetic and copies ran while one was open for 3% -> 0% of each run, Pallas kernels for 0% -> 0%
where the time goes in v2:
time: 130 us; the launch traced here: 129 us
  Pallas kernels  125 us (96%)
  local copies, waits for them, and re-layouts  3.49 us (3%)
    pallas_call x1, Pallas kernels, body(): pl.pallas_call(kernel, out_shape=jax.ShapeDtypeStruct((2 * per, cells), f...  125 us

profile of v2, /device:TPU:8, one launch (start us, length us, event | category | flops | bytes accessed | tf_op | source)
XLA Modules:
  0.0 128.6 jit_solution(11972018761325052566)
XLA Ops:
  0.0 1.6 %copy.14 = bf16[2,8,4096]{2,1,0:T(8,128)(2,1)} copy(bf16[2,8,4096]{2,0,1:T(2,128)(2,1)} %bitcast.18) | data formatting | bytes 262144 | tf_op jit(solution)/shard_map/transpose | solution.py:383
  1.6 125.1 %shard_map.82 = f32[16,4096]{1,0:T(8,128)} custom-call(s32[1,4]{1,0:T(1,128)} %bt_ref.1, bf16[16,4096]{1,0:T(8,128)(2,1)} %bitcast.16, bf16[2,4096,128]{2,1,0:T(8,128)(2,1)} %bitcast.14, bf16[2,128,512]{2,1,0:T(8,128)(2,1)} %bitcast.17, s32[1,128]{1,0:T(1,128)} %bins_ref.1, s32[32,512]{1,0:T(8,128)} %wedge_ref.1, bf16[1024,512]{1,0:T(8,128)(2,1)} %constant.4.clone.thi_ref, ...), custom_call_target="tpu_custom_call" | custom-call | tf_op jit(solution)/shard_map/pallas_call | solution.py:389
  126.8 1.9 %copy.13 = f32[2,8,4096]{2,0,1:T(2,128)} copy(f32[2,8,4096]{2,1,0:T(8,128)} %bitcast.15) | data formatting | bytes 524288 | tf_op jit(solution)/shard_map/reshape | solution.py:431

commit v3 on v2

v3 whole, which is shorter than its diff:
```python
import functools
import math

import jax
import jax.numpy as jnp
import numpy as np
from jax import lax
from jax.experimental import pallas as pl
from jax.experimental.pallas import tpu as pltpu
from jax.sharding import Mesh
from jax.sharding import PartitionSpec as P

FREQ = ("freq_0", "freq_1", "freq_2")
AXES = ("tile",) + FREQ
RING = 4
ROWS = 16
GATHER_SHAPE = (
    (
        (1, -1, -1, 1, 1, -1, 1, -1),
        (-1, -1, 1, -1, -1, -1, -1, 1),
        (1, 1, -1, -1, 1, 1, -1, -1),
        (1, 1, -1, 1, -1, 1, -1, -1),
    ),
    {(0, "F"): -1, (10, "A"): 1, (10, "B"): -1, (11, "A"): 1, (14, "B"): 1},
)
REDUCE_SHAPE = (
    (
        (1, 1, -1, -1, 1, -1, 1, -1),
        (1, 1, -1, -1, 1, 1, 1, -1),
        (1, -1, -1, -1, 1, -1, -1, 1),
        (-1, 1, 1, 1, 1, -1, -1, -1),
    ),
    {(0, "F"): -1, (10, "A"): -1, (10, "B"): 1, (11, "A"): 1, (14, "B"): -1},
)
SERVE = (
    0, 3, 12, 36, 9, 17, 16, 41, 48, 22, 24, 19, 144, 23, 47, 6, 29, 46, 40, 84, 28, 34, 96, 60,
    180, 35, 51, 44, 57, 147, 43, 156, 178, 82, 20, 132, 94, 108, 153, 88, 31, 188, 168, 105, 72,
    89, 99, 65, 184, 64, 130, 70, 32, 92, 190, 54, 79, 142, 175, 160, 71, 185, 166, 118, 167, 136,
    95, 119, 80, 161, 113, 112, 191, 77, 150, 140, 143, 68, 172, 91, 120, 179, 137, 128, 102, 127,
    76, 173, 176, 187, 131, 67, 83, 163, 139, 125, 164, 115, 116, 124,
)
ISSUE = (
    144, 48, 9, 3, 12, 36, 17, 41, 16, 22, 40, 24, 46, 47, 6, 23, 29, 19, 60, 51, 96, 57, 84, 34,
    28, 180, 147, 156, 153, 35, 20, 44, 43, 88, 94, 31, 178, 82, 105, 108, 132, 99, 70, 72, 64,
    190, 184, 168, 65, 54, 89, 32, 92, 188, 95, 71, 185, 161, 160, 166, 130, 120, 136, 142, 112,
    118, 150, 191, 167, 91, 79, 175, 140, 172, 143, 119, 102, 76, 113, 137, 77, 67, 176, 80, 187,
    68, 127, 173, 163, 115, 179, 139, 83, 131, 128, 164, 124, 125, 116,
)
RETURN = (
    125, 140, 116, 115, 119, 131, 118, 127, 124, 187, 137, 139, 113, 173, 102, 143, 128, 163, 112,
    172, 80, 188, 120, 142, 185, 68, 164, 136, 179, 99, 79, 105, 176, 83, 108, 77, 76, 190, 166,
    67, 184, 82, 132, 91, 150, 94, 161, 130, 168, 167, 160, 54, 191, 175, 89, 92, 72, 96, 64, 88,
    65, 32, 95, 147, 71, 70, 156, 180, 153, 51, 60, 31, 84, 57, 43, 46, 178, 47, 19, 20, 144, 29,
    44, 48, 34, 28, 35, 6, 41, 22, 16, 17, 24, 40, 23, 9, 12, 3, 36, 0,
)
GROUPS = (16, 16, 16, 8, 8)


def at(dx, dy):
    return (dx % RING) * RING + dy % RING


def decoded(code):
    return code // 48, code // 3 % 16, "FAB"[code % 3]


def message_tree(shape):
    sides, by_z = shape
    kids = {}

    def edge(parent, axis, step, child):
        if axis == "z" or not (child[0] and child[1:] in by_z):
            kids.setdefault(parent, []).append((axis, step, child))

    for what, side in by_z.items():
        edge((0, *what), "z", -1, (1, *what))
        edge((0, *what), "z", 1, (3, *what))
        edge((2 + side, *what), "z", side, (2, *what))
    for dz in range(RING):
        for turn, part in (("y", "A"), ("x", "B")):
            axis, first = ("x", 0) if part == "A" else ("y", RING)

            def cell(along, across):
                return at(along, across) if axis == "x" else at(across, along)

            side = sides[dz][0]
            for step in (1, -1):
                edge((dz, 0, "F"), axis, step, (dz, cell(-step, 0), "F"))
            edge((dz, cell(-side, 0), "F"), axis, side, (dz, cell(2, 0), "F"))
            for d in range(1, RING):
                for step in (1, -1):
                    edge((dz, cell(d, 0), "F"), turn, step, (dz, cell(d, -step), part))
                side_d = sides[dz][first + d]
                edge((dz, cell(d, -side_d), part), turn, side_d, (dz, cell(d, 2), part))
    return kids


def parents(kids):
    return {child: (axis, step) for edges in kids.values() for axis, step, child in edges}


DOWN = message_tree(GATHER_SHAPE)
for edges in DOWN.values():
    edges.sort(key=lambda edge: ISSUE.index((edge[2][0] * 16 + edge[2][1]) * 3 + "FAB".index(edge[2][2])))
UP = message_tree(REDUCE_SHAPE)
SERVED_BY = parents(DOWN)
RETURNED_BY = parents(UP)
SEMAPHORE = {message: n for n, message in enumerate(SERVED_BY)}
HALVES = {m: n for n, m in enumerate(m for m in SERVED_BY if m[2] != "F")}
FULLS = {m: n for n, m in enumerate(m for m in SERVED_BY if m[2] == "F" and m[1])}


def kernel(
    bt_ref, sky_ref, ker_ref, data_ref, bins_ref, wedge_ref, thi_ref, tlo_ref, out_ref,
    buf, kc, acc, vp, t1r, hs, hr, vis, spec, vhi, vlo, mask, dat, u, g,
    rs_h, rs_f, zs, zr, raw_sky, raw, wedge, thi, tlo,
    local_sem, send_sem, ag_sem, rs_sem, t_send, t_recv,
):
    tile = lax.axis_index("tile")
    y = lax.axis_index("freq_0")
    z = lax.axis_index("freq_1")
    x = lax.axis_index("freq_2")
    cells = sky_ref.shape[2]
    half = cells // 2
    chans, base = vis.shape[1], vis.shape[2]
    per = chans // RING**3
    core = lax.rem(tile, 2)
    mate = tile + 1 - 2 * core

    def near(axis, step):
        if axis == "x":
            return (tile, y, z, lax.rem(x + step + RING, RING))
        if axis == "y":
            return (tile, lax.rem(y + step + RING, RING), z, x)
        return (tile, y, lax.rem(z + step + RING, RING), x)

    over = lax.rem(tile + 2, 4)
    cross = lax.rem(mate + 2, 4)
    peers = [near("x", 1), near("x", -1), near("y", 1), near("y", -1)]
    peers += [near("z", 1), near("z", -1)]
    peers += [(t, y, z, x) for t in (mate, over, cross)]

    load_sky = pltpu.make_async_copy(sky_ref, raw_sky, local_sem.at[0])
    load_r = pltpu.make_async_copy(ker_ref.at[0], kc.at[:, 0:base], local_sem.at[1])
    load_i = pltpu.make_async_copy(ker_ref.at[1], kc.at[:, base : 2 * base], local_sem.at[2])
    load_sky.start()
    late = [load_r, load_i]
    for n, (src, dst) in enumerate(
        ((wedge_ref, wedge), (data_ref, raw), (thi_ref, thi), (tlo_ref, tlo))
    ):
        late.append(pltpu.make_async_copy(src, dst, local_sem.at[3 + n]))
    barrier = pltpu.get_barrier_semaphore()
    for peer in peers:
        pl.semaphore_signal(barrier, inc=1, device_id=peer, device_id_type=pl.DeviceIdType.MESH)
    for load in late:
        load.start()
    load_sky.wait()
    buf[0, 0] = jnp.concatenate(
        [raw_sky[:, plane, :].astype(jnp.float32) for plane in range(2)], axis=0
    ).astype(jnp.bfloat16)
    pl.semaphore_wait(barrier, len(peers))

    def part_of(ref, dz, cell, part):
        if part == "F":
            return ref.at[dz, cell]
        lo = 0 if part == "A" else half
        return ref.at[dz, cell, :, lo : lo + half]

    def remote(src, dst, send, recv, peer):
        return pltpu.make_async_remote_copy(
            src_ref=src, dst_ref=dst, send_sem=send, recv_sem=recv,
            device_id=peer, device_id_type=pl.DeviceIdType.MESH,
        )

    weight = bt_ref[0, tile].astype(jnp.float32)

    sent = []

    def gather_serve(key):
        if key in SERVED_BY:
            ref = part_of(buf, *key)
            remote(ref, ref, send_sem.at[0], ag_sem.at[SEMAPHORE[key]], near("x", 1)).wait_recv()
        for axis, step, child in DOWN.get(key, ()):
            copy = remote(
                part_of(buf, *key[:2], child[2]), part_of(buf, *child),
                send_sem.at[SEMAPHORE[child]], ag_sem.at[SEMAPHORE[child]], near(axis, step),
            )
            copy.start()
            sent.append(copy)

    depth = 512
    deep = cells // depth

    def forward(shards, place):
        count = len(shards)
        rows = pl.ds(0, count * ROWS)
        acc[rows, :] = jnp.zeros((count * ROWS, 2 * base), jnp.float32)

        @pl.loop(0, deep)
        def _(k):
            lanes = pl.ds(pl.multiple_of(k * depth, depth), depth)
            value = jnp.concatenate([buf[dz, cell, :, lanes] for dz, cell in shards], axis=0)
            acc[rows, :] += jnp.dot(value, kc[lanes, :], preferred_element_type=jnp.float32)

        out = acc[rows, :].reshape(count, 2, per, 2 * base)
        real = out[:, 0, :, :base] - out[:, 1, :, base:]
        imag = out[:, 1, :, :base] + out[:, 0, :, base:]
        vp[0, place, :] = (real * weight).reshape(count * per, base)
        vp[1, place, :] = (imag * weight).reshape(count * per, base)

    def t1(n, place):
        return remote(vp.at[1 - core, place], t1r.at[place], t_send.at[n, 0], t_recv.at[n, 0],
                      (mate, y, z, x))

    def t2(n, place):
        return [
            remote(hs.at[place], hr.at[k, place], t_send.at[n, k + 1], t_recv.at[n, k + 1],
                   (t, y, z, x))
            for k, t in enumerate((over, cross, mate))
        ]

    def row_of(dz, cell):
        sx = lax.rem(x + cell // RING, RING)
        sy = lax.rem(y + cell % RING, RING)
        sz = lax.rem(z + dz, RING)
        return pl.multiple_of((sy * RING * RING + sz * RING + sx) * per, per)

    def tile_1(n, shards, place):
        forward(shards, place)
        t1(n, place).start()

    def tile_2(n, shards, place):
        t1(n, place).wait_recv()
        hs[place, :] = vp[core, place, :] + t1r[place, :]
        for copy in t2(n, place):
            copy.start()

    def tile_3(n, shards, place):
        for copy in t2(n, place):
            copy.wait_recv()
        for k, shard in enumerate(shards):
            mine = slice(place.start + k * per, place.start + (k + 1) * per)
            rows = pl.ds(row_of(*shard), per)
            vis[core, rows, :] = hs[mine, :] + hr[0, mine, :]
            vis[1 - core, rows, :] = hr[2, mine, :] + hr[1, mine, :]

    def prepare():
        for load in late:
            load.wait()
        levels = lax.broadcasted_iota(jnp.int32, (wedge.shape[0], base), 0)
        hot = (levels == bins_ref[...]).astype(jnp.bfloat16)
        keep = wedge[...].astype(jnp.float32).T.astype(jnp.bfloat16)
        mask[...] = jnp.dot(keep, hot, preferred_element_type=jnp.float32)
        for plane in range(2):
            dat[plane] = raw[plane].astype(jnp.float32).T

    serve = [decoded(code) for code in SERVE]
    whole = {}
    for n, key in enumerate(serve):
        whole[key[:2]] = n
    order = sorted(whole, key=whole.get)
    plan = {n: [functools.partial(gather_serve, key)] for n, key in enumerate(serve)}
    plan[4].append(prepare)
    groups = []
    start = 0
    for n, count in enumerate(GROUPS):
        shards = order[start : start + count]
        groups.append((n, shards, slice(start * per, (start + count) * per)))
        start += count
        last = max(whole[shard] for shard in shards)
        final = n == len(GROUPS) - 1
        for work, lag in ((tile_1, 0), (tile_2, 8), (tile_3, 24)):
            spot = last + lag if not final else len(serve) + lag
            plan.setdefault(spot, []).append(functools.partial(work, *groups[-1]))
    for spot in sorted(plan):
        for step in plan[spot]:
            step()
    for copy in sent:
        copy.wait_send()
    for n, _, place in groups:
        for copy in (t1(n, place), *t2(n, place)):
            copy.wait_send()

    norm = 1.0 / math.sqrt(chans)
    block = 256

    def transform():
        for plane in range(2):
            lanes = slice(plane * base, (plane + 1) * base)
            whole = vis[plane]
            vhi[:, lanes] = whole.astype(jnp.bfloat16)
            vlo[:, lanes] = (whole - vhi[:, lanes].astype(jnp.float32)).astype(jnp.bfloat16)

        @pl.loop(0, 2 * chans // block)
        def _(n):
            rows = pl.ds(pl.multiple_of(n * block, block), block)
            spec[rows, :] = (
                jnp.dot(thi[rows, :], vhi[...], preferred_element_type=jnp.float32)
                + jnp.dot(thi[rows, :], vlo[...], preferred_element_type=jnp.float32)
                + jnp.dot(tlo[rows, :], vhi[...], preferred_element_type=jnp.float32)
            )

    cos_rows, sin_rows = slice(0, chans), slice(chans, 2 * chans)
    lane_r, lane_i = slice(0, base), slice(base, 2 * base)
    transform()
    vis[0] = mask[...] * (
        (spec[cos_rows, lane_r] + spec[sin_rows, lane_i]) * norm - dat[0]
    )
    vis[1] = mask[...] * (
        (spec[cos_rows, lane_i] - spec[sin_rows, lane_r]) * norm - dat[1]
    )
    transform()
    vis[0] = (spec[cos_rows, lane_r] - spec[sin_rows, lane_i]) * (norm * weight)
    vis[1] = (spec[cos_rows, lane_i] + spec[sin_rows, lane_r]) * (norm * weight)
    for dz in range(RING):
        for cell in range(RING * RING):
            rows = pl.ds(row_of(dz, cell), per)
            ur, ui = vis[0, rows, :], vis[1, rows, :]
            top = jnp.concatenate([ur, ui], axis=1)
            low = jnp.concatenate([ui, -ur], axis=1)
            u[dz, cell] = jnp.concatenate([top, low], axis=0).astype(jnp.bfloat16)

    def backward(dz, part):
        rows = u[dz].reshape(RING * RING * ROWS, 2 * base)
        first = 0 if part == "A" else deep // 2

        @pl.loop(first, first + deep // 2)
        def _(k):
            lanes = pl.ds(pl.multiple_of(k * depth, depth), depth)
            value = lax.dot_general(
                rows, kc[lanes, :], (((1,), (1,)), ((), ())),
                preferred_element_type=jnp.float32,
            )
            g[dz, :, :, lanes] = value.reshape(RING * RING, ROWS, depth)

    width = 1024

    def total(dst, dz, cell, part, terms):
        start = half if part == "B" else 0
        stop = half if part == "A" else cells

        def step_of(n):
            lanes = pl.ds(pl.multiple_of(start + n * width, width), width)
            value = g[dz, cell, :, lanes]
            for ref, kind in terms:
                shift = half if kind == "B" else 0
                own = pl.ds(pl.multiple_of(start - shift + n * width, width), width)
                value = value + ref[:, own].astype(jnp.float32)
            dst[:, lanes] = value.astype(dst.dtype)

        pl.loop(0, (stop - start) // width)(step_of)

    def returned(key):
        dz, cell, part = key
        axis, step = RETURNED_BY[key]
        if cell == 0 and dz and axis == "z":
            src, dst = zs.at[dz - 1], zr.at[dz - 1]
        else:
            src = part_of(buf, *key)
            dst = rs_f.at[FULLS[key]] if part == "F" else rs_h.at[HALVES[key]]
        n = SEMAPHORE[key]
        return remote(src, dst, send_sem.at[n], rs_sem.at[n], near(axis, -step)), src, dst

    ready = set()
    for code in RETURN:
        key = decoded(code)
        dz, cell, part = key
        root = key not in RETURNED_BY
        for half_part in "AB" if part == "F" else part:
            if (dz, half_part) not in ready:
                ready.add((dz, half_part))
                backward(dz, half_part)
        got = []
        for _, _, child in UP.get(key, ()):
            copy, _, dst = returned(child)
            copy.wait_recv()
            got.append((dst, child[2]))
        whole = out_ref if root else zs.at[dz - 1] if cell == 0 else buf.at[dz, cell]
        kinds = {kind for _, kind in got}
        if part == "F" and kinds - {"F"}:
            for half_part in "AB":
                total(whole, dz, cell, half_part, [t for t in got if t[1] in ("F", half_part)])
        else:
            total(whole, dz, cell, part, got)
        if not root:
            returned(key)[0].start()
    for key in RETURNED_BY:
        returned(key)[0].wait_send()


def delay_tables(length):
    indices = np.arange(length, dtype=np.int64)
    angle = (indices[:, None] * indices[None, :] % length) * (2.0 * np.pi / length)
    table = np.concatenate([np.cos(angle), np.sin(angle)], axis=0).astype(np.float32)
    high = table.astype(jnp.bfloat16)
    low = (table - high.astype(np.float32)).astype(jnp.bfloat16)
    return high, low


def body(sky, ker, data, block_tiles, length_bin, wedge_keep):
    per, cells = sky.shape[1], sky.shape[3]
    chans, base = data.shape[3], data.shape[2]
    high, low = delay_tables(chans)
    full = RING * RING
    vmem = pl.BlockSpec(memory_space=pltpu.VMEM)
    hbm = pl.BlockSpec(memory_space=pl.ANY)
    f32, bf16 = jnp.float32, jnp.bfloat16
    out = pl.pallas_call(
        kernel,
        out_shape=jax.ShapeDtypeStruct((2 * per, cells), f32),
        in_specs=[pl.BlockSpec(memory_space=pltpu.SMEM), hbm, hbm, hbm, vmem, hbm, hbm, hbm],
        out_specs=vmem,
        scratch_shapes=[
            pltpu.VMEM((RING, full, ROWS, cells), bf16),
            pltpu.VMEM((cells, 2 * base), bf16),
            pltpu.VMEM((full * ROWS, 2 * base), f32),
            pltpu.VMEM((2, chans, base), f32),
            pltpu.VMEM((chans, base), f32),
            pltpu.VMEM((chans, base), f32),
            pltpu.VMEM((3, chans, base), f32),
            pltpu.VMEM((2, chans, base), f32),
            pltpu.VMEM((2 * chans, 2 * base), f32),
            pltpu.VMEM((chans, 2 * base), bf16),
            pltpu.VMEM((chans, 2 * base), bf16),
            pltpu.VMEM((chans, base), f32),
            pltpu.VMEM((2, chans, base), f32),
            pltpu.VMEM((RING, full, ROWS, 2 * base), bf16),
            pltpu.VMEM((RING, full, ROWS, cells), f32),
            pltpu.VMEM((len(HALVES), ROWS, cells // 2), bf16),
            pltpu.VMEM((len(FULLS), ROWS, cells), bf16),
            pltpu.VMEM((RING - 1, ROWS, cells), f32),
            pltpu.VMEM((RING - 1, ROWS, cells), f32),
            pltpu.VMEM((per, 2, cells), bf16),
            pltpu.VMEM((2, base, chans), bf16),
            pltpu.VMEM(wedge_keep.shape, jnp.int32),
            pltpu.VMEM((2 * chans, chans), bf16),
            pltpu.VMEM((2 * chans, chans), bf16),
            pltpu.SemaphoreType.DMA((7,)),
            pltpu.SemaphoreType.DMA((len(SEMAPHORE),)),
            pltpu.SemaphoreType.DMA((len(SEMAPHORE),)),
            pltpu.SemaphoreType.DMA((len(SEMAPHORE),)),
            pltpu.SemaphoreType.DMA((len(GROUPS), 4)),
            pltpu.SemaphoreType.DMA((len(GROUPS), 4)),
        ],
        compiler_params=pltpu.CompilerParams(
            collective_id=0, has_side_effects=True, vmem_limit_bytes=60 * 2**20
        ),
    )(block_tiles, sky[0], ker[0, 0], data[0], length_bin, wedge_keep, high, low)
    return jnp.transpose(out.reshape(2, per, cells), (1, 0, 2))[None]


def solution(mesh):
    finer = Mesh(mesh.devices.reshape(mesh.shape["tile"], RING, RING, RING), AXES)
    return jax.shard_map(
        body,
        mesh=finer,
        in_specs=(
            P("tile", FREQ, None, None),
            P("tile", FREQ, None, None, None),
            P(FREQ, None, None, None),
            P(FREQ, None),
            P(FREQ, None),
            P(),
        ),
        out_specs=P("tile", FREQ, None, None),
        check_vma=False,
    )
```

time: 130 us -> 124 us (0.954)
  Pallas kernels: 125 us -> 122 us
  local copies, waits for them, and re-layouts: 3.49 us -> 1.86 us
    pallas_call x1, Pallas kernels: 125 us -> 122 us  [body(): pl.pallas_call(kernel, out_shape=jax.ShapeDtypeStruct((2 * per, cells), f...]
    transpose x1 -> x0, local copies, waits for them, and re-layouts: 1.64 us -> none  [body(): shard = jnp.transpose(sky[0], (1, 0, 2)).reshape(2 * per, cells)]
where the time goes in v3:
time: 124 us
  Pallas kernels  122 us (98%)
  local copies, waits for them, and re-layouts  1.86 us (2%)
    pallas_call x1, Pallas kernels, body(): pl.pallas_call(kernel, out_shape=jax.ShapeDtypeStruct((2 * per, cells), f...  122 us

profile of v3, /device:TPU:8, one launch (start us, length us, event | category | flops | bytes accessed | tf_op | source)
XLA Modules:
  0.0 123.5 jit_solution(14248451561613018554)
XLA Ops:
  0.0 121.7 %shard_map.82 = f32[16,4096]{1,0:T(8,128)} custom-call(s32[1,4]{1,0:T(1,128)} %bt_ref.1, bf16[8,2,4096]{2,1,0:T(2,128)(2,1)} %bitcast.12, bf16[2,4096,128]{2,1,0:T(8,128)(2,1)} %bitcast.9, bf16[2,128,512]{2,1,0:T(8,128)(2,1)} %bitcast.11, s32[1,128]{1,0:T(1,128)} %bins_ref.1, s32[32,512]{1,0:T(8,128)} %wedge_ref.1, bf16[1024,512]{1,0:T(8,128)(2,1)} %constant.4.clone.thi_ref, ...), custom_call_target="tpu_custom_call" | custom-call | tf_op jit(solution)/shard_map/pallas_call | solution.py:408
  121.7 1.9 %copy.11 = f32[2,8,4096]{2,0,1:T(2,128)} copy(f32[2,8,4096]{2,1,0:T(8,128)} %bitcast.10) | data formatting | bytes 524288 | tf_op jit(solution)/shard_map/reshape | solution.py:449

commit v4 on v3

--- a/solution.py
+++ b/solution.py
@@ -16,44 +16,45 @@
 ROWS = 16
 GATHER_SHAPE = (
     (
-        (1, -1, -1, 1, 1, -1, 1, -1),
-        (-1, -1, 1, -1, -1, -1, -1, 1),
-        (1, 1, -1, -1, 1, 1, -1, -1),
-        (1, 1, -1, 1, -1, 1, -1, -1),
+        (1, 1, -1, -1, -1, 1, 1, -1),
+        (-1, 1, 1, 1, -1, -1, -1, -1),
+        (1, 1, 1, -1, 1, -1, -1, 1),
+        (1, -1, -1, -1, -1, -1, 1, 1),
     ),
     {(0, "F"): -1, (10, "A"): 1, (10, "B"): -1, (11, "A"): 1, (14, "B"): 1},
 )
 REDUCE_SHAPE = (
     (
-        (1, 1, -1, -1, 1, -1, 1, -1),
-        (1, 1, -1, -1, 1, 1, 1, -1),
-        (1, -1, -1, -1, 1, -1, -1, 1),
-        (-1, 1, 1, 1, 1, -1, -1, -1),
+        (1, -1, -1, 1, 1, -1, 1, -1),
+        (1, -1, -1, 1, -1, 1, -1, -1),
+        (1, 1, 1, 1, 1, 1, -1, 1),
+        (-1, -1, -1, -1, -1, -1, -1, -1),
     ),
-    {(0, "F"): -1, (10, "A"): -1, (10, "B"): 1, (11, "A"): 1, (14, "B"): -1},
+    {(0, "F"): -1, (10, "A"): 1, (10, "B"): 1, (11, "A"): -1, (14, "B"): 1},
 )
 SERVE = (
-    0, 3, 12, 36, 9, 17, 16, 41, 48, 22, 24, 19, 144, 23, 47, 6, 29, 46, 40, 84, 28, 34, 96, 60,
-    180, 35, 51, 44, 57, 147, 43, 156, 178, 82, 20, 132, 94, 108, 153, 88, 31, 188, 168, 105, 72,
-    89, 99, 65, 184, 64, 130, 70, 32, 92, 190, 54, 79, 142, 175, 160, 71, 185, 166, 118, 167, 136,
-    95, 119, 80, 161, 113, 112, 191, 77, 150, 140, 143, 68, 172, 91, 120, 179, 137, 128, 102, 127,
-    76, 173, 176, 187, 131, 67, 83, 163, 139, 125, 164, 115, 116, 124,
+    0, 9, 36, 3, 12, 23, 40, 48, 6, 24, 35, 43, 144, 22, 47, 16, 17, 41, 46, 57, 51, 20, 28, 44,
+    -16, 96, 34, 156, 60, -32, 153, 84, 71, 29, 19, 54, 147, 180, 31, 89, 108, 188, -48, 82, 65,
+    166, 32, 99, 105, -64, 95, 92, 160, 178, 70, -17, 167, 132, 175, 150, 191, 79, 72, -33, 64,
+    94, 185, 68, 140, 83, 190, 161, 88, 112, 118, 168, 163, 80, 184, 176, 137, 77, 113, 136, -18,
+    143, 119, 102, 130, -34, 164, 172, 67, 120, 173, 128, 142, 76, 187, -49, 127, 91, 179, -19,
+    125, 139, -65, -50, 115, 131, 116, 124, -20, -35, -66, -36, -51, -52, -67, -68,
 )
 ISSUE = (
-    144, 48, 9, 3, 12, 36, 17, 41, 16, 22, 40, 24, 46, 47, 6, 23, 29, 19, 60, 51, 96, 57, 84, 34,
-    28, 180, 147, 156, 153, 35, 20, 44, 43, 88, 94, 31, 178, 82, 105, 108, 132, 99, 70, 72, 64,
-    190, 184, 168, 65, 54, 89, 32, 92, 188, 95, 71, 185, 161, 160, 166, 130, 120, 136, 142, 112,
-    118, 150, 191, 167, 91, 79, 175, 140, 172, 143, 119, 102, 76, 113, 137, 77, 67, 176, 80, 187,
-    68, 127, 173, 163, 115, 179, 139, 83, 131, 128, 164, 124, 125, 116,
+    48, 9, 36, 3, 12, 144, 6, 23, 47, 40, 46, 24, 17, 41, 22, 16, 35, 43, 60, 96, 51, 84, 57, 20,
+    44, 34, 28, 147, 180, 153, 156, 19, 29, 71, 95, 65, 89, 54, 31, 92, 188, 32, 105, 99, 108,
+    132, 178, 82, 160, 166, 70, 72, 64, 191, 150, 167, 94, 88, 83, 68, 185, 161, 184, 168, 190,
+    79, 175, 112, 118, 140, 77, 80, 176, 137, 113, 119, 102, 143, 163, 130, 67, 142, 120, 136,
+    127, 164, 179, 76, 91, 173, 115, 172, 128, 187, 125, 139, 131, 116, 124,
 )
 RETURN = (
-    125, 140, 116, 115, 119, 131, 118, 127, 124, 187, 137, 139, 113, 173, 102, 143, 128, 163, 112,
-    172, 80, 188, 120, 142, 185, 68, 164, 136, 179, 99, 79, 105, 176, 83, 108, 77, 76, 190, 166,
-    67, 184, 82, 132, 91, 150, 94, 161, 130, 168, 167, 160, 54, 191, 175, 89, 92, 72, 96, 64, 88,
-    65, 32, 95, 147, 71, 70, 156, 180, 153, 51, 60, 31, 84, 57, 43, 46, 178, 47, 19, 20, 144, 29,
-    44, 48, 34, 28, 35, 6, 41, 22, 16, 17, 24, 40, 23, 9, 12, 3, 36, 0,
+    125, 124, 116, 112, 115, 113, 68, 139, 131, 179, 130, 83, 127, 137, 136, 120, 118, 119, 128,
+    76, 80, 142, 187, 102, 79, 143, 172, 77, 91, 173, 82, 99, 132, 108, 105, 67, 140, 191, 89,
+    167, 163, 164, 65, 176, 190, 72, 71, 92, 54, 88, 70, 184, 64, 95, 161, 160, 96, 168, 178, 94,
+    32, 185, 175, 166, 150, 51, 57, 60, 84, 188, 153, 156, 180, 47, 147, 43, 44, 31, 34, 22, 19,
+    29, 20, 48, 144, 41, 28, 35, 16, 6, 46, 17, 24, 40, 23, 12, 3, 9, 36, 0,
 )
-GROUPS = (16, 16, 16, 8, 8)
+GROUPS = (16, 16, 16, 12, 4)
 
 
 def at(dx, dy):
@@ -95,13 +96,17 @@
     return kids
 
 
+def coded(message):
+    return (message[0] * 16 + message[1]) * 3 + "FAB".index(message[2])
+
+
 def parents(kids):
     return {child: (axis, step) for edges in kids.values() for axis, step, child in edges}
 
 
 DOWN = message_tree(GATHER_SHAPE)
 for edges in DOWN.values():
-    edges.sort(key=lambda edge: ISSUE.index((edge[2][0] * 16 + edge[2][1]) * 3 + "FAB".index(edge[2][2])))
+    edges.sort(key=lambda edge: ISSUE.index(coded(edge[2])))
 UP = message_tree(REDUCE_SHAPE)
 SERVED_BY = parents(DOWN)
 RETURNED_BY = parents(UP)
@@ -112,7 +117,7 @@
 
 def kernel(
     bt_ref, sky_ref, ker_ref, data_ref, bins_ref, wedge_ref, thi_ref, tlo_ref, out_ref,
-    buf, kc, acc, vp, t1r, hs, hr, vis, spec, vhi, vlo, mask, dat, u, g,
+    buf, kc, acc, vp, t1r, hs, hr, tt, tr, vis, spec, vhi, vlo, mask, dat, u, g,
     rs_h, rs_f, zs, zr, raw_sky, raw, wedge, thi, tlo,
     local_sem, send_sem, ag_sem, rs_sem, t_send, t_recv,
 ):
@@ -135,10 +140,9 @@
         return (tile, y, lax.rem(z + step + RING, RING), x)
 
     over = lax.rem(tile + 2, 4)
-    cross = lax.rem(mate + 2, 4)
     peers = [near("x", 1), near("x", -1), near("y", 1), near("y", -1)]
     peers += [near("z", 1), near("z", -1)]
-    peers += [(t, y, z, x) for t in (mate, over, cross)]
+    peers += [(t, y, z, x) for t in (mate, over)]
 
     load_sky = pltpu.make_async_copy(sky_ref, raw_sky, local_sem.at[0])
     load_r = pltpu.make_async_copy(ker_ref.at[0], kc.at[:, 0:base], local_sem.at[1])
@@ -213,11 +217,12 @@
                       (mate, y, z, x))
 
     def t2(n, place):
-        return [
-            remote(hs.at[place], hr.at[k, place], t_send.at[n, k + 1], t_recv.at[n, k + 1],
-                   (t, y, z, x))
-            for k, t in enumerate((over, cross, mate))
-        ]
+        return remote(hs.at[place], hr.at[place], t_send.at[n, 1], t_recv.at[n, 1],
+                      (over, y, z, x))
+
+    def t3(n, place):
+        return remote(tt.at[place], tr.at[place], t_send.at[n, 2], t_recv.at[n, 2],
+                      (mate, y, z, x))
 
     def row_of(dz, cell):
         sx = lax.rem(x + cell // RING, RING)
@@ -232,17 +237,20 @@
     def tile_2(n, shards, place):
         t1(n, place).wait_recv()
         hs[place, :] = vp[core, place, :] + t1r[place, :]
-        for copy in t2(n, place):
-            copy.start()
+        t2(n, place).start()
 
     def tile_3(n, shards, place):
-        for copy in t2(n, place):
-            copy.wait_recv()
+        t2(n, place).wait_recv()
+        tt[place, :] = hs[place, :] + hr[place, :]
+        t3(n, place).start()
+
+    def tile_4(n, shards, place):
+        t3(n, place).wait_recv()
         for k, shard in enumerate(shards):
             mine = slice(place.start + k * per, place.start + (k + 1) * per)
             rows = pl.ds(row_of(*shard), per)
-            vis[core, rows, :] = hs[mine, :] + hr[0, mine, :]
-            vis[1 - core, rows, :] = hr[2, mine, :] + hr[1, mine, :]
+            vis[core, rows, :] = tt[mine, :]
+            vis[1 - core, rows, :] = tr[mine, :]
 
     def prepare():
         for load in late:
@@ -254,31 +262,28 @@
         for plane in range(2):
             dat[plane] = raw[plane].astype(jnp.float32).T
 
-    serve = [decoded(code) for code in SERVE]
     whole = {}
-    for n, key in enumerate(serve):
-        whole[key[:2]] = n
+    for n, code in enumerate(SERVE):
+        if code >= 0:
+            whole[decoded(code)[:2]] = n
     order = sorted(whole, key=whole.get)
-    plan = {n: [functools.partial(gather_serve, key)] for n, key in enumerate(serve)}
-    plan[4].append(prepare)
     groups = []
     start = 0
     for n, count in enumerate(GROUPS):
-        shards = order[start : start + count]
-        groups.append((n, shards, slice(start * per, (start + count) * per)))
+        place = slice(start * per, (start + count) * per)
+        groups.append((n, order[start : start + count], place))
         start += count
-        last = max(whole[shard] for shard in shards)
-        final = n == len(GROUPS) - 1
-        for work, lag in ((tile_1, 0), (tile_2, 8), (tile_3, 24)):
-            spot = last + lag if not final else len(serve) + lag
-            plan.setdefault(spot, []).append(functools.partial(work, *groups[-1]))
-    for spot in sorted(plan):
-        for step in plan[spot]:
-            step()
+    for n, code in enumerate(SERVE):
+        if code >= 0:
+            gather_serve(decoded(code))
+        else:
+            (tile_1, tile_2, tile_3, tile_4)[-code // 16 - 1](*groups[-code % 16])
+        if n == 4:
+            prepare()
     for copy in sent:
         copy.wait_send()
     for n, _, place in groups:
-        for copy in (t1(n, place), *t2(n, place)):
+        for copy in (t1(n, place), t2(n, place), t3(n, place)):
             copy.wait_send()
 
     norm = 1.0 / math.sqrt(chans)
@@ -417,7 +422,9 @@
             pltpu.VMEM((2, chans, base), f32),
             pltpu.VMEM((chans, base), f32),
             pltpu.VMEM((chans, base), f32),
-            pltpu.VMEM((3, chans, base), f32),
+            pltpu.VMEM((chans, base), f32),
+            pltpu.VMEM((chans, base), f32),
+            pltpu.VMEM((chans, base), f32),
             pltpu.VMEM((2, chans, base), f32),
             pltpu.VMEM((2 * chans, 2 * base), f32),
             pltpu.VMEM((chans, 2 * base), bf16),
@@ -439,8 +446,8 @@
             pltpu.SemaphoreType.DMA((len(SEMAPHORE),)),
             pltpu.SemaphoreType.DMA((len(SEMAPHORE),)),
             pltpu.SemaphoreType.DMA((len(SEMAPHORE),)),
-            pltpu.SemaphoreType.DMA((len(GROUPS), 4)),
-            pltpu.SemaphoreType.DMA((len(GROUPS), 4)),
+            pltpu.SemaphoreType.DMA((len(GROUPS), 3)),
+            pltpu.SemaphoreType.DMA((len(GROUPS), 3)),
         ],
         compiler_params=pltpu.CompilerParams(
             collective_id=0, has_side_effects=True, vmem_limit_bytes=60 * 2**20

time: 124 us -> 117 us (0.944)
  Pallas kernels: 122 us -> 114 us
    pallas_call x1, Pallas kernels: 122 us -> 114 us  [body(): pl.pallas_call(kernel, out_shape=jax.ShapeDtypeStruct((2 * per, cells), f...]
where the time goes in v4:
time: 117 us; the launch traced here: 116 us
  Pallas kernels  114 us (97%)
  local copies, waits for them, and re-layouts  1.86 us (2%)
    pallas_call x1, Pallas kernels, body(): pl.pallas_call(kernel, out_shape=jax.ShapeDtypeStruct((2 * per, cells), f...  114 us

profile of v4, /device:TPU:8, one launch (start us, length us, event | category | flops | bytes accessed | tf_op | source)
XLA Modules:
  0.0 115.9 jit_solution(9270879052685835252)
XLA Ops:
  0.0 114.1 %shard_map.82 = f32[16,4096]{1,0:T(8,128)} custom-call(s32[1,4]{1,0:T(1,128)} %bt_ref.1, bf16[8,2,4096]{2,1,0:T(2,128)(2,1)} %bitcast.12, bf16[2,4096,128]{2,1,0:T(8,128)(2,1)} %bitcast.9, bf16[2,128,512]{2,1,0:T(8,128)(2,1)} %bitcast.11, s32[1,128]{1,0:T(1,128)} %bins_ref.1, s32[32,512]{1,0:T(8,128)} %wedge_ref.1, bf16[1024,512]{1,0:T(8,128)(2,1)} %constant.4.clone.thi_ref, ...), custom_call_target="tpu_custom_call" | custom-call | tf_op jit(solution)/shard_map/pallas_call | solution.py:413
  114.1 1.9 %copy.11 = f32[2,8,4096]{2,0,1:T(2,128)} copy(f32[2,8,4096]{2,1,0:T(8,128)} %bitcast.10) | data formatting | bytes 524288 | tf_op jit(solution)/shard_map/reshape | solution.py:456

commit v5 on v4

--- a/solution.py
+++ b/solution.py
@@ -48,11 +48,11 @@
     127, 164, 179, 76, 91, 173, 115, 172, 128, 187, 125, 139, 131, 116, 124,
 )
 RETURN = (
-    125, 124, 116, 112, 115, 113, 68, 139, 131, 179, 130, 83, 127, 137, 136, 120, 118, 119, 128,
-    76, 80, 142, 187, 102, 79, 143, 172, 77, 91, 173, 82, 99, 132, 108, 105, 67, 140, 191, 89,
-    167, 163, 164, 65, 176, 190, 72, 71, 92, 54, 88, 70, 184, 64, 95, 161, 160, 96, 168, 178, 94,
-    32, 185, 175, 166, 150, 51, 57, 60, 84, 188, 153, 156, 180, 47, 147, 43, 44, 31, 34, 22, 19,
-    29, 20, 48, 144, 41, 28, 35, 16, 6, 46, 17, 24, 40, 23, 12, 3, 9, 36, 0,
+    116, 125, 124, 115, 130, 68, 131, 128, 136, 112, 139, 137, 113, 172, 118, 80, 83, 76, 127,
+    120, 173, 163, 119, 142, 143, 99, 176, 102, 77, 79, 82, 92, 65, 108, 91, 164, 95, 67, 71, 132,
+    105, 89, 54, 72, 178, 187, 140, 160, 88, 179, 96, 70, 94, 191, 64, 161, 168, 150, 190, 166,
+    57, 167, 185, 175, 32, 184, 51, 60, 84, 188, 147, 153, 180, 34, 31, 43, 156, 20, 44, 19, 47,
+    48, 144, 35, 28, 41, 22, 6, 29, 40, 16, 23, 46, 24, 17, 12, 9, 3, 36, 0,
 )
 GROUPS = (16, 16, 16, 12, 4)
 
@@ -117,7 +117,7 @@
 
 def kernel(
     bt_ref, sky_ref, ker_ref, data_ref, bins_ref, wedge_ref, thi_ref, tlo_ref, out_ref,
-    buf, kc, acc, vp, t1r, hs, hr, tt, tr, vis, spec, vhi, vlo, mask, dat, u, g,
+    buf, kc, vp, t1r, hs, hr, tt, tr, vis, spec, vhi, vlo, mask, dat, u, g,
     rs_h, rs_f, zs, zr, raw_sky, raw, wedge, thi, tlo,
     local_sem, send_sem, ag_sem, rs_sem, t_send, t_recv,
 ):
@@ -192,21 +192,12 @@
             copy.start()
             sent.append(copy)
 
-    depth = 512
-    deep = cells // depth
 
     def forward(shards, place):
         count = len(shards)
-        rows = pl.ds(0, count * ROWS)
-        acc[rows, :] = jnp.zeros((count * ROWS, 2 * base), jnp.float32)
-
-        @pl.loop(0, deep)
-        def _(k):
-            lanes = pl.ds(pl.multiple_of(k * depth, depth), depth)
-            value = jnp.concatenate([buf[dz, cell, :, lanes] for dz, cell in shards], axis=0)
-            acc[rows, :] += jnp.dot(value, kc[lanes, :], preferred_element_type=jnp.float32)
-
-        out = acc[rows, :].reshape(count, 2, per, 2 * base)
+        value = jnp.concatenate([buf[dz, cell] for dz, cell in shards], axis=0)
+        out = jnp.dot(value, kc[...], preferred_element_type=jnp.float32)
+        out = out.reshape(count, 2, per, 2 * base)
         real = out[:, 0, :, :base] - out[:, 1, :, base:]
         imag = out[:, 1, :, :base] + out[:, 0, :, base:]
         vp[0, place, :] = (real * weight).reshape(count * per, base)
@@ -287,7 +278,6 @@
             copy.wait_send()
 
     norm = 1.0 / math.sqrt(chans)
-    block = 256
 
     def transform():
         for plane in range(2):
@@ -296,14 +286,11 @@
             vhi[:, lanes] = whole.astype(jnp.bfloat16)
             vlo[:, lanes] = (whole - vhi[:, lanes].astype(jnp.float32)).astype(jnp.bfloat16)
 
-        @pl.loop(0, 2 * chans // block)
-        def _(n):
-            rows = pl.ds(pl.multiple_of(n * block, block), block)
-            spec[rows, :] = (
-                jnp.dot(thi[rows, :], vhi[...], preferred_element_type=jnp.float32)
-                + jnp.dot(thi[rows, :], vlo[...], preferred_element_type=jnp.float32)
-                + jnp.dot(tlo[rows, :], vhi[...], preferred_element_type=jnp.float32)
-            )
+        spec[...] = (
+            jnp.dot(thi[...], vhi[...], preferred_element_type=jnp.float32)
+            + jnp.dot(thi[...], vlo[...], preferred_element_type=jnp.float32)
+            + jnp.dot(tlo[...], vhi[...], preferred_element_type=jnp.float32)
+        )
 
     cos_rows, sin_rows = slice(0, chans), slice(chans, 2 * chans)
     lane_r, lane_i = slice(0, base), slice(base, 2 * base)
@@ -317,7 +304,8 @@
     transform()
     vis[0] = (spec[cos_rows, lane_r] - spec[sin_rows, lane_i]) * (norm * weight)
     vis[1] = (spec[cos_rows, lane_i] + spec[sin_rows, lane_r]) * (norm * weight)
-    for dz in range(RING):
+
+    def assemble(dz):
         for cell in range(RING * RING):
             rows = pl.ds(row_of(dz, cell), per)
             ur, ui = vis[0, rows, :], vis[1, rows, :]
@@ -327,16 +315,11 @@
 
     def backward(dz, part):
         rows = u[dz].reshape(RING * RING * ROWS, 2 * base)
-        first = 0 if part == "A" else deep // 2
-
-        @pl.loop(first, first + deep // 2)
-        def _(k):
-            lanes = pl.ds(pl.multiple_of(k * depth, depth), depth)
-            value = lax.dot_general(
-                rows, kc[lanes, :], (((1,), (1,)), ((), ())),
-                preferred_element_type=jnp.float32,
-            )
-            g[dz, :, :, lanes] = value.reshape(RING * RING, ROWS, depth)
+        lanes = slice(0, half) if part == "A" else slice(half, cells)
+        value = lax.dot_general(
+            rows, kc[lanes, :], (((1,), (1,)), ((), ())), preferred_element_type=jnp.float32
+        )
+        g[dz, :, :, lanes] = value.reshape(RING * RING, ROWS, half)
 
     width = 1024
 
@@ -351,7 +334,11 @@
                 shift = half if kind == "B" else 0
                 own = pl.ds(pl.multiple_of(start - shift + n * width, width), width)
                 value = value + ref[:, own].astype(jnp.float32)
-            dst[:, lanes] = value.astype(dst.dtype)
+            if dst is out_ref:
+                for plane in range(2):
+                    dst[:, plane, lanes] = value[plane * per : (plane + 1) * per]
+            else:
+                dst[:, lanes] = value.astype(dst.dtype)
 
         pl.loop(0, (stop - start) // width)(step_of)
 
@@ -373,6 +360,8 @@
         root = key not in RETURNED_BY
         for half_part in "AB" if part == "F" else part:
             if (dz, half_part) not in ready:
+                if not ready & {(dz, "A"), (dz, "B")}:
+                    assemble(dz)
                 ready.add((dz, half_part))
                 backward(dz, half_part)
         got = []
@@ -412,13 +401,12 @@
     f32, bf16 = jnp.float32, jnp.bfloat16
     out = pl.pallas_call(
         kernel,
-        out_shape=jax.ShapeDtypeStruct((2 * per, cells), f32),
+        out_shape=jax.ShapeDtypeStruct((per, 2, cells), f32),
         in_specs=[pl.BlockSpec(memory_space=pltpu.SMEM), hbm, hbm, hbm, vmem, hbm, hbm, hbm],
         out_specs=vmem,
         scratch_shapes=[
             pltpu.VMEM((RING, full, ROWS, cells), bf16),
             pltpu.VMEM((cells, 2 * base), bf16),
-            pltpu.VMEM((full * ROWS, 2 * base), f32),
             pltpu.VMEM((2, chans, base), f32),
             pltpu.VMEM((chans, base), f32),
             pltpu.VMEM((chans, base), f32),
@@ -453,7 +441,7 @@
             collective_id=0, has_side_effects=True, vmem_limit_bytes=60 * 2**20
         ),
     )(block_tiles, sky[0], ker[0, 0], data[0], length_bin, wedge_keep, high, low)
-    return jnp.transpose(out.reshape(2, per, cells), (1, 0, 2))[None]
+    return out[None]
 
 
 def solution(mesh):

time: 117 us -> 114 us (0.974)
  Pallas kernels: 114 us -> 112 us
    pallas_call x1, Pallas kernels: 114 us -> 112 us  [body(): pl.pallas_call(kernel, out_shape=jax.ShapeDtypeStruct((per, 2, cells), f3...]
    reshape x1 -> x0, local copies, waits for them, and re-layouts: 1.86 us -> none  [body(): return jnp.transpose(out.reshape(2, per, cells), (1, 0, 2))[None]]
    unnamed x0 -> x1, local copies, waits for them, and re-layouts: none -> 1.67 us
where the time goes in v5:
time: 114 us; the launch traced here: 113 us
  Pallas kernels  112 us (98%)
  local copies, waits for them, and re-layouts  1.67 us (1%)
    pallas_call x1, Pallas kernels, body(): pl.pallas_call(kernel, out_shape=jax.ShapeDtypeStruct((per, 2, cells), f3...  112 us

profile of v5, /device:TPU:8, one launch (start us, length us, event | category | flops | bytes accessed | tf_op | source)
XLA Modules:
  0.0 113.3 jit_solution(4541649157347992264)
XLA Ops:
  0.0 111.6 %shard_map.82 = f32[8,2,4096]{2,1,0:T(2,128)} custom-call(s32[1,4]{1,0:T(1,128)} %bt_ref.1, bf16[8,2,4096]{2,1,0:T(2,128)(2,1)} %bitcast.7, bf16[2,4096,128]{2,1,0:T(8,128)(2,1)} %bitcast.4, bf16[2,128,512]{2,1,0:T(8,128)(2,1)} %bitcast.6, s32[1,128]{1,0:T(1,128)} %bins_ref.1, s32[32,512]{1,0:T(8,128)} %wedge_ref.1, ...), custom_call_target="tpu_custom_call" | custom-call | tf_op jit(solution)/shard_map/pallas_call | solution.py:402
  111.6 1.7 %copy.10 = f32[1,8,2,4096]{3,2,1,0:T(2,128)} copy(f32[1,8,2,4096]{3,2,1,0:T(2,128)} %bitcast.5) | data formatting | bytes 524288
